TPU v7x, 32 devices: a whole 2x2x4 slice. The times are simulated.
32 devices in a mesh: panel: 4 (over y, core), tile: 4 (over z), lev: 2 (over x).
Axes of the slice: x: 2, y: 2, z: 4, core: 2. Of those that a mesh axis runs over, the one named last changes fastest.
Arguments:
- adjoint_new: float32 [5, 16, 32768], P(None, 'lev', ('panel', 'tile')), may hold values from -6 to 6
- weights: float32 [4, 32768], P(None, ('panel', 'tile', 'lev')), may hold values from 0.05 to 0.5
- departure: int32 [4, 32768], P(None, ('panel', 'tile')), may hold values from 0 to 2047
- send_point: int32 [4, 2048], P(None, ('panel', 'tile')), may hold values from 0 to 8191, as said below
- block_count: int32 [4, 16], P(None, ('panel', 'tile')), may hold values from 0 to 128, as said below
- rotation: int32 [2, 16], P(None, ('panel', 'tile')), may hold values from 0 to 3
Outputs:
- adjoint_old: float32 [5, 16, 32768], P(None, 'lev', ('panel', 'tile'))
Inputs may be any that keep to these rules, and one draw needn't show every extreme that they name: `send_point`: within one tile the 512 entries are distinct stencil point numbers k * 2048 + c of that tile's own cells. `block_count`: zero for block 0 on the first tile and for block 1 on the last tile of each sector; every block position reaches 128 on some tile in every draw.
All inputs are finite; a program needn't handle non-finite values.
Results may differ from a plain program's by a relative error of at most 0.00002.
Values sent between devices are 32-bit elements; how exact they have to be, the bound alone decides.
No kernel may reach another device: no remote copies, remote signals or barrier semaphores. Data moves between devices by JAX's collectives and lax.ppermute only.
A program may use at most 64 MiB of HBM per device.

v0:
```python
import jax
import jax.numpy as jnp
from jax import lax
from jax.sharding import PartitionSpec as P


def shifted(block, axis, distance):
    devices = range(lax.axis_size(axis))
    route = [(i - distance, i) for i in devices if i - distance in devices]
    return lax.ppermute(block, axis, route)


def shifted_2(value, axis, steps):
    count = lax.axis_size(axis)
    pairs = [(source, (source + steps) % count) for source in range(count)]
    return lax.ppermute(value, axis, pairs)


def quarter_turn(turn_code):
    cosine = (turn_code == 0).astype(jnp.float32) - (turn_code == 2).astype(jnp.float32)
    sine_term = (turn_code == 1).astype(jnp.float32) - (turn_code == 3).astype(jnp.float32)
    return (cosine, sine_term)


def body(adjoint_new, weights, departure, send_point, block_count, rotation):
    fields, levels, cell_count = adjoint_new.shape
    blocks, slot_count = send_point.shape
    stencil = departure.shape[0]
    row_count = fields * levels
    points = stencil * cell_count
    weight_full = lax.all_gather(weights, "lev", axis=1, tiled=True)
    weighted = (adjoint_new[:, :, None, :] * weight_full[None, None, :, :]).reshape(
        row_count, points
    )
    chosen = send_point.reshape(-1)
    live_mask = lax.broadcasted_iota(jnp.int32, (blocks, slot_count), 1) < block_count
    picked = weighted[:, chosen].reshape(fields, levels, blocks, slot_count) * live_mask.astype(
        jnp.float32
    )
    cosine, sine_term = quarter_turn(rotation)
    zonal_part = picked[0, :, 2:, :]
    merid_part = picked[1, :, 2:, :]
    turned_zonal = cosine * zonal_part + sine_term * merid_part
    turned_merid = cosine * merid_part - sine_term * zonal_part
    wind_rows = jnp.stack(
        [
            jnp.concatenate([picked[0, :, :2, :], turned_zonal], axis=1),
            jnp.concatenate([picked[1, :, :2, :], turned_merid], axis=1),
        ]
    )
    outgoing = jnp.concatenate([wind_rows, picked[2:]], axis=0).reshape(
        row_count, blocks, slot_count
    )
    targets = departure.reshape(-1)[chosen].reshape(blocks, slot_count)
    dropped = jnp.where(live_mask, send_point, points).reshape(-1)
    keep_local = jnp.ones((points,), jnp.float32).at[dropped].set(0.0, mode="drop")
    result = (
        jnp.zeros((row_count, cell_count), jnp.float32)
        .at[:, departure.reshape(-1)]
        .add(weighted * keep_local)
    )
    from_before = shifted((outgoing[:, 1], targets[1]), "tile", 1)
    from_beyond = shifted((outgoing[:, 0], targets[0]), "tile", -1)
    seam_before = shifted_2((outgoing[:, 3], targets[3]), "panel", 1)
    seam_beyond = shifted_2((outgoing[:, 2], targets[2]), "panel", -1)
    received = (from_before, from_beyond, seam_before, seam_beyond)
    arrived = jnp.concatenate([member[0] for member in received], axis=1)
    arrived_ids = jnp.concatenate([member[1] for member in received])
    result = result.at[:, arrived_ids].add(arrived)
    return result.reshape(fields, levels, cell_count)


def solution(mesh):
    return jax.shard_map(
        body,
        mesh=mesh,
        in_specs=(
            P(None, "lev", ("panel", "tile")),
            P(None, ("panel", "tile", "lev")),
            P(None, ("panel", "tile")),
            P(None, ("panel", "tile")),
            P(None, ("panel", "tile")),
            P(None, ("panel", "tile")),
        ),
        out_specs=P(None, "lev", ("panel", "tile")),
        check_vma=False,
    )
```

profile of v0, /device:TPU:0, one launch (start us, length us, event | category | flops | bytes accessed | tf_op | source)
XLA Modules:
  0.0 89.8 jit_solution(12144871391484140187)
XLA Ops:
  0.0 0.0 copy-start
  0.0 0.8 fusion.4
  0.8 0.8 fusion.5
  1.5 0.0 copy-done
  1.5 0.3 broadcast_bitcast_fusion
  1.9 0.0 copy-start.2
  1.9 0.7 copy.26
  2.7 0.0 copy-done.2
  2.7 5.3 %all_gather.3 = f32[4,2048]{1,0:T(4,128)S(1)} all-gather(f32[4,1024]{1,0:T(4,128)S(1)} %copy-done.2), channel_id=1, replica_groups=mesh['panel'=4,'tile'=4,'lev'=2] {'lev'}, dimensions={1}, use_global_device_ids=true | all-gather | bytes 49152 | tf_op jit(solution)/shard_map/all_gather | solution.py:31
  8.0 2.5 %scatter_custom_fusion = f32[8192]{0:T(1024)S(1)} fusion(s32[512]{0:T(512)S(1)} %bitcast.80, f32[512]{0:T(512)S(1)} %broadcast.90, f32[]{:T(128)} %constant.11.clone.1), kind=kCustom, calls=%fused_computation.21 | custom fusion | bytes 32772 | tf_op jit(solution)/shard_map/scatter | solution.py:56
  10.5 1.3 %multiply_bitcast_fusion = (f32[8192,40]{0,1:T(8,128)S(1)}, f32[40,8192]{1,0:T(8,128)}) fusion(f32[8192]{0:T(1024)S(1)} %scatter_custom_fusion, f32[40,8192]{1,0:T(8,128)S(1)} %bitcast.66, f32[8192]{0:T(1024)S(1)} %bitcast.68), kind=kLoop, calls=%fused_computation.5 | loop fusion | flops 655360 | bytes 3997696 | tf_op jit(solution)/shard_map/mul | solution.py:60
  11.8 0.0 copy-start.3
  11.8 3.7 %copy.20 = f32[40,8192]{0,1:T(8,128)} copy(f32[40,8192]{1,0:T(8,128)} %get-tuple-element.6) | data formatting | bytes 2621440 | tf_op jit(solution)/shard_map/mul | solution.py:32
  15.4 0.0 copy-start.4
  15.4 0.0 copy-start.1
  15.5 0.0 copy-done.3
  15.5 3.2 %gather_fusion.1 = f32[512,40]{1,0:T(8,128)S(1)} fusion(f32[40,8192]{0,1:T(8,128)} %copy.20, s32[1024]{0:T(1024)S(1)} %pad_clamp_fusion), kind=kCustom, calls=%fused_computation.1 | custom fusion | bytes 165888 | tf_op jit(solution)/shard_map/gather | solution.py:37
  18.7 0.1 copy.21
  18.9 0.0 copy-done.4
  18.9 0.1 multiply_add_fusion
  19.0 4.0 %collective-permute-start.4 = (f32[40,128]{1,0:T(8,128)S(1)}, f32[40,128]{1,0:T(8,128)S(1)}, u32[]{:S(2)}, u32[]{:S(2)}) collective-permute-start(f32[40,128]{1,0:T(8,128)S(1)} %get-tuple-element.9), channel_id=1, source_target_pairs={{0,2},{2,4},{4,6},{1,3},{3,5},{5,7},{8,10},{10,12},{12,14},{9,11},... | collective-permute-start | bytes 61448 | tf_op jit(solution)/shard_map/ppermute | solution.py:10
  23.0 0.0 copy-done.1
  23.1 3.1 %gather_fusion = s32[512]{0:T(512)S(1)} fusion(s32[8192]{0:T(1024)S(1)} %bitcast.65, s32[1024]{0:T(1024)S(1)} %pad_clamp_fusion), kind=kCustom, calls=%fused_computation | custom fusion | bytes 6144 | tf_op jit(solution)/shard_map/gather | solution.py:54
  26.2 0.1 collective-permute-start.3
  26.3 3.5 %collective-permute-start = (s32[128]{0:T(128)S(1)}, s32[128]{0:T(128)S(1)}, u32[]{:S(2)}, u32[]{:S(2)}) collective-permute-start(s32[128]{0:T(128)S(1)} %get-tuple-element.15), channel_id=1, source_target_pairs={{0,2},{2,4},{4,6},{1,3},{3,5},{5,7},{8,10},{10,12},{12,14},{9,11},... | collective-permute-start | bytes 1544 | tf_op jit(solution)/shard_map/ppermute | solution.py:10
  29.8 1.3 %collective-permute-start.1 = (s32[128]{0:T(128)S(1)}, s32[128]{0:T(128)S(1)}, u32[]{:S(2)}, u32[]{:S(2)}) collective-permute-start(s32[128]{0:T(128)S(1)} %get-tuple-element.17), channel_id=1, source_target_pairs={{2,0},{4,2},{6,4},{3,1},{5,3},{7,5},{10,8},{12,10},{14,12},{11,9},... | collective-permute-start | bytes 1544 | tf_op jit(solution)/shard_map/ppermute | solution.py:10
  31.1 0.3 collective-permute-start.2
  31.4 2.7 %copy.19 = f32[8192,40]{1,0:T(8,128)} copy(f32[8192,40]{0,1:T(8,128)S(1)} %get-tuple-element.5) | data formatting | bytes 2621440 | tf_op jit(solution)/shard_map/mul | solution.py:60
  34.1 44.6 %scatter_custom_fusion.1 = f32[40,2048]{0,1:T(8,128)S(1)} fusion(s32[8192]{0:T(1024)S(1)} %bitcast.73, f32[8192,40]{1,0:T(8,128)} %copy.19, f32[]{:T(128)} %constant.8.clone.1), kind=kCustom, calls=%fused_computation.8 | custom fusion | flops 327680 | bytes 328192 | tf_op jit(solution)/shard_map/scatter-add | solution.py:60
  78.7 0.0 collective-permute-done.3
  78.7 1.3 %collective-permute-start.5 = (f32[40,128]{1,0:T(8,128)S(1)}, f32[40,128]{1,0:T(8,128)S(1)}, u32[]{:S(2)}, u32[]{:S(2)}) collective-permute-start(f32[40,128]{1,0:T(8,128)S(1)} %get-tuple-element.12), channel_id=1, source_target_pairs={{2,0},{4,2},{6,4},{3,1},{5,3},{7,5},{10,8},{12,10},{14,12},{11,9},... | collective-permute-start | bytes 61448 | tf_op jit(solution)/shard_map/ppermute | solution.py:10
  80.0 0.0 collective-permute-done
  80.0 1.5 %collective-permute-start.6 = (f32[40,128]{1,0:T(8,128)S(1)}, f32[40,128]{1,0:T(8,128)S(1)}, u32[]{:S(2)}, u32[]{:S(2)}) collective-permute-start(f32[40,128]{1,0:T(8,128)S(1)} %get-tuple-element.11), channel_id=1, source_target_pairs={{0,8},{8,16},{16,24},{24,0},{1,9},{9,17},{17,25},{25,1},{2,10},{10... | collective-permute-start | bytes 61448 | tf_op jit(solution)/shard_map/ppermute | solution.py:16
  81.5 0.0 collective-permute-done.1
  81.5 0.3 collective-permute-start.7
  81.8 0.0 collective-permute-done.2
  81.8 0.0 collective-permute-done.4
  81.8 3.0 %collective-permute-done.5 = f32[40,128]{1,0:T(8,128)S(1)} collective-permute-done((f32[40,128]{1,0:T(8,128)S(1)}, f32[40,128]{1,0:T(8,128)S(1)}, u32[]{:S(2)}, u32[]{:S(2)}) %collective-permute-start.5) | collective-permute-done | bytes 20512 | tf_op jit(solution)/shard_map/ppermute | solution.py:10
  84.8 0.0 collective-permute-done.6
  84.8 0.0 collective-permute-done.7
  84.8 0.1 copy.23
  84.9 3.9 %scatter_fusion = f32[40,2048]{0,1:T(8,128)S(1)} fusion(f32[40,2048]{0,1:T(8,128)S(1)} %scatter_custom_fusion.1, s32[512]{0:T(512)S(1)} %bitcast.74, f32[512,40]{1,0:T(8,128)S(1)} %copy.23), kind=kCustom, calls=%fused_computation.4 | custom fusion | flops 20480 | bytes 247808 | tf_op jit(solution)/shard_map/scatter-add | solution.py:69
  88.8 1.0 %copy.24 = f32[40,2048]{1,0:T(8,128)} copy(f32[40,2048]{0,1:T(8,128)S(1)} %scatter_fusion) | data formatting | bytes 655360 | tf_op jit(solution)/shard_map/scatter-add | solution.py:69
  (18 shorter events, 0.2 us)
Async XLA Ops:
  0.0 1.5 %copy-start = (f32[5,8,2048]{2,1,0:T(8,128)S(1)}, f32[5,8,2048]{2,1,0:T(8,128)}, u32[]{:S(2)}) copy-start(f32[5,8,2048]{2,1,0:T(8,128)} %param.6) | copy-start | bytes 983044
  1.9 0.8 copy-start.2
  11.8 3.7 %copy-start.3 = (s32[4,128]{1,0:T(4,128)S(1)}, s32[4,128]{1,0:T(4,128)}, u32[]{:S(2)}) copy-start(s32[4,128]{1,0:T(4,128)} %param.9) | copy-start | bytes 6148
  15.4 3.4 %copy-start.4 = (s32[2,1]{0,1:T(1,128)S(1)}, s32[2,1]{0,1:T(1,128)}, u32[]{:S(2)}) copy-start(s32[2,1]{0,1:T(1,128)} %param.11) | copy-start | bytes 28
  15.4 7.6 %copy-start.1 = (s32[4,2048]{1,0:T(4,128)S(1)}, s32[4,2048]{1,0:T(4,128)}, u32[]{:S(2)}) copy-start(s32[4,2048]{1,0:T(4,128)} %param.8) | copy-start | bytes 98308
  19.0 62.8 %collective-permute-start.4 = (f32[40,128]{1,0:T(8,128)S(1)}, f32[40,128]{1,0:T(8,128)S(1)}, u32[]{:S(2)}, u32[]{:S(2)}) collective-permute-start(f32[40,128]{1,0:T(8,128)S(1)} %get-tuple-element.9), channel_id=1, source_target_pairs={{0,2},{2,4},{4,6},{1,3},{3,5},{5,7},{8,10},{10,12},{12,14},{9,11},... | collective-permute-start | bytes 61448 | tf_op jit(solution)/shard_map/ppermute | solution.py:10
  26.2 52.4 %collective-permute-start.3 = (s32[128]{0:T(128)S(1)}, s32[128]{0:T(128)S(1)}, u32[]{:S(2)}, u32[]{:S(2)}) collective-permute-start(s32[128]{0:T(128)S(1)} %get-tuple-element.18), channel_id=1, source_target_pairs={{0,24},{8,0},{16,8},{24,16},{1,25},{9,1},{17,9},{25,17},{2,26},{10... | collective-permute-start | bytes 1544 | tf_op jit(solution)/shard_map/ppermute | solution.py:16
  26.3 53.7 %collective-permute-start = (s32[128]{0:T(128)S(1)}, s32[128]{0:T(128)S(1)}, u32[]{:S(2)}, u32[]{:S(2)}) collective-permute-start(s32[128]{0:T(128)S(1)} %get-tuple-element.15), channel_id=1, source_target_pairs={{0,2},{2,4},{4,6},{1,3},{3,5},{5,7},{8,10},{10,12},{12,14},{9,11},... | collective-permute-start | bytes 1544 | tf_op jit(solution)/shard_map/ppermute | solution.py:10
  29.8 51.7 %collective-permute-start.1 = (s32[128]{0:T(128)S(1)}, s32[128]{0:T(128)S(1)}, u32[]{:S(2)}, u32[]{:S(2)}) collective-permute-start(s32[128]{0:T(128)S(1)} %get-tuple-element.17), channel_id=1, source_target_pairs={{2,0},{4,2},{6,4},{3,1},{5,3},{7,5},{10,8},{12,10},{14,12},{11,9},... | collective-permute-start | bytes 1544 | tf_op jit(solution)/shard_map/ppermute | solution.py:10
  31.1 50.7 %collective-permute-start.2 = (s32[128]{0:T(128)S(1)}, s32[128]{0:T(128)S(1)}, u32[]{:S(2)}, u32[]{:S(2)}) collective-permute-start(s32[128]{0:T(128)S(1)} %get-tuple-element.16), channel_id=1, source_target_pairs={{0,8},{8,16},{16,24},{24,0},{1,9},{9,17},{17,25},{25,1},{2,10},{10... | collective-permute-start | bytes 1544 | tf_op jit(solution)/shard_map/ppermute | solution.py:16
  78.7 6.1 %collective-permute-start.5 = (f32[40,128]{1,0:T(8,128)S(1)}, f32[40,128]{1,0:T(8,128)S(1)}, u32[]{:S(2)}, u32[]{:S(2)}) collective-permute-start(f32[40,128]{1,0:T(8,128)S(1)} %get-tuple-element.12), channel_id=1, source_target_pairs={{2,0},{4,2},{6,4},{3,1},{5,3},{7,5},{10,8},{12,10},{14,12},{11,9},... | collective-permute-start | bytes 61448 | tf_op jit(solution)/shard_map/ppermute | solution.py:10
  80.0 4.8 %collective-permute-start.6 = (f32[40,128]{1,0:T(8,128)S(1)}, f32[40,128]{1,0:T(8,128)S(1)}, u32[]{:S(2)}, u32[]{:S(2)}) collective-permute-start(f32[40,128]{1,0:T(8,128)S(1)} %get-tuple-element.11), channel_id=1, source_target_pairs={{0,8},{8,16},{16,24},{24,0},{1,9},{9,17},{17,25},{25,1},{2,10},{10... | collective-permute-start | bytes 61448 | tf_op jit(solution)/shard_map/ppermute | solution.py:16
  81.5 3.3 %collective-permute-start.7 = (f32[40,128]{1,0:T(8,128)S(1)}, f32[40,128]{1,0:T(8,128)S(1)}, u32[]{:S(2)}, u32[]{:S(2)}) collective-permute-start(f32[40,128]{1,0:T(8,128)S(1)} %get-tuple-element.10), channel_id=1, source_target_pairs={{0,24},{8,0},{16,8},{24,16},{1,25},{9,1},{17,9},{25,17},{2,26},{10... | collective-permute-start | bytes 61448 | tf_op jit(solution)/shard_map/ppermute | solution.py:16
where the time goes:
time: 90.9 us; the launch traced here: 89.8 us
  other arithmetic  51.4 us (57%)
  local copies, waits for them, and re-layouts  17.6 us (19%)
  starting transfers between devices  12.2 us (13%)
  blocking collectives  5.33 us (6%)
  waiting for transfers between devices  3 us (3%)
    scatter-add x1, other arithmetic, body(): result = jnp.zeros((row_count, cell_count), jnp.float32).at[:, departure....  44.6 us
    ppermute x4, starting transfers between devices, shifted(): return lax.ppermute(block, axis, route)  10.1 us
    all_gather x1, blocking collectives, body(): weight_full = lax.all_gather(weights, 'lev', axis=1, tiled=True)  5.33 us
    scatter-add x1, other arithmetic, body(): result = result.at[:, arrived_ids].add(arrived)  3.87 us
    mul x1, local copies, waits for them, and re-layouts, body(): adjoint_new[:, :, None, :] * weight_full[None, None, :, :]  3.66 us
    gather x2, local copies, waits for them, and re-layouts, body(): weighted[:, chosen].reshape(fields, levels, blocks, slot_count)  3.32 us
    gather x1, local copies, waits for them, and re-layouts, body(): targets = departure.reshape(-1)[chosen].reshape(blocks, slot_count)  3.14 us
    ppermute x4, waiting for transfers between devices, shifted(): return lax.ppermute(block, axis, route)  2.99 us
  transfers between devices with their start and end apart: 8, of which 1 were waited for; matrix products, arithmetic and copies ran while one was open for 56% of the time, Pallas kernels for 0%

commit v1 on v0

v1 whole, which is shorter than its diff:
```python
import jax
import jax.numpy as jnp
from jax import lax
from jax.experimental import pallas as pl
from jax.experimental.pallas import tpu as pltpu
from jax.sharding import PartitionSpec as P

F32, BF16, I32 = jnp.float32, jnp.bfloat16, jnp.int32
LO = 256
LANES = 128
SUB = 8
VMEM = pl.BlockSpec(memory_space=pltpu.VMEM)
SMEM = pl.BlockSpec(memory_space=pltpu.SMEM)
PARAMS = pltpu.CompilerParams(vmem_limit_bytes=32 << 20)


def two_terms(value):
    high = value.astype(BF16).astype(F32)
    return jnp.concatenate([high, value - high], axis=0)


def place_weights(parts, full):
    count = len(parts)
    width = parts[0].shape[1]
    me = lax.axis_index("lev")
    for s, part in enumerate(parts):
        source = lax.rem(me + (count - s), count)
        full[:, pl.ds(pl.multiple_of(source * width, LANES), width)] = part[...]


def scatter_product(terms, target, cells):
    points = target.shape[1]
    high = target // LO
    low = target - high * LO
    left = jnp.concatenate(
        [terms * (high == h).astype(F32).astype(BF16) for h in range(cells // LO)], axis=0
    )
    lane = lax.broadcasted_iota(I32, (LO, points), 0)
    right = (lane == low).astype(F32).astype(BF16)
    return lax.dot_general(
        left, right, (((1,), (1,)), ((), ())), preferred_element_type=F32
    )


def pick_kernel(count, levels, u_ref, dep_ref, sp_ref, bc_ref, rot_ref, *refs):
    parts, outs, full = refs[:count], refs[count:-1], refs[-1]
    rows, cells = u_ref.shape
    stencil = dep_ref.shape[0]
    blocks, slots = sp_ref.shape
    place_weights(parts, full)
    dep = dep_ref[...]
    dep_high = dep // SUB
    dep_low = dep - dep_high * SUB
    w = full[...]
    w0 = w.astype(BF16).astype(F32)
    w1 = (w - w0).astype(BF16).astype(F32)
    table = jnp.concatenate(
        [
            two_terms(u_ref[...]),
            jnp.concatenate([dep_high.astype(F32), dep_low.astype(F32)], axis=0),
            jnp.concatenate([w0, w1], axis=0),
            jnp.concatenate([w - w0 - w1, jnp.zeros_like(w)], axis=0),
            jnp.zeros((SUB, cells), F32),
        ],
        axis=0,
    ).astype(BF16)
    chosen = [sp_ref[j : j + 1, :] for j in range(blocks)]
    which = [c // cells for c in chosen]
    column = jnp.concatenate([c - k * cells for c, k in zip(chosen, which)], axis=1)
    cell = lax.broadcasted_iota(I32, (cells, blocks * slots), 0)
    onehot = (cell == column).astype(F32).astype(BF16)
    got = jnp.dot(table, onehot, preferred_element_type=F32)
    slot = lax.broadcasted_iota(I32, (1, slots), 1)
    d0 = 2 * rows
    w0 = d0 + 2 * stencil
    for j in range(blocks):
        g = got[:, j * slots : (j + 1) * slots]
        ids = jnp.zeros((1, slots), F32)
        weight = jnp.zeros((1, slots), F32)
        for k in range(stencil):
            hit = which[j] == k
            one_id = g[d0 + k : d0 + k + 1] * SUB + g[d0 + stencil + k : d0 + stencil + k + 1]
            one_w = (
                g[w0 + k : w0 + k + 1]
                + g[w0 + stencil + k : w0 + stencil + k + 1]
                + g[w0 + 2 * stencil + k : w0 + 2 * stencil + k + 1]
            )
            ids = ids + jnp.where(hit, one_id, 0.0)
            weight = weight + jnp.where(hit, one_w, 0.0)
        weight = jnp.where(slot < bc_ref[j], weight, 0.0)
        values = (g[:rows] + g[rows : 2 * rows]) * weight
        zonal, merid = values[:levels], values[levels : 2 * levels]
        if j >= 2:
            code = rot_ref[j - 2]
            cosine = (code == 0).astype(F32) - (code == 2).astype(F32)
            sine = (code == 1).astype(F32) - (code == 3).astype(F32)
            zonal, merid = cosine * zonal + sine * merid, cosine * merid - sine * zonal
        out = outs[j]
        out[:levels, :] = zonal
        out[levels : 2 * levels, :] = merid
        out[2 * levels : rows, :] = values[2 * levels :]
        out[rows:, :] = jnp.broadcast_to(ids, (SUB, slots))


def local_kernel(count, u_ref, dep_ref, sp_ref, bc_ref, *refs):
    parts, out_ref, full, acc = refs[:count], refs[-3], refs[-2], refs[-1]
    rows, cells = u_ref.shape
    stencil = dep_ref.shape[0]
    blocks, slots = sp_ref.shape
    tiles = cells // LANES
    place_weights(parts, full)
    slot = lax.broadcasted_iota(I32, (1, slots), 1)
    codes, lanes = [], []
    for j in range(blocks):
        chosen = sp_ref[j : j + 1, :]
        which = chosen // cells
        column = chosen - which * cells
        tile = column // LANES
        codes.append(jnp.where(slot < bc_ref[j], tile * SUB + which, -1))
        lanes.append(column - tile * LANES)
    shape = (tiles * SUB, blocks * slots)
    row = lax.broadcasted_iota(I32, shape, 0)
    left = (row == jnp.concatenate(codes, axis=1)).astype(F32).astype(BF16)
    lane_row = lax.broadcasted_iota(I32, (LANES, blocks * slots), 0)
    right = (lane_row == jnp.concatenate(lanes, axis=1)).astype(F32).astype(BF16)
    sent = lax.dot_general(
        left, right, (((1,), (1,)), ((), ())), preferred_element_type=F32
    )
    for t in range(tiles):
        at = slice(t * LANES, (t + 1) * LANES)
        full[:, at] = full[:, at] * (1.0 - sent[t * SUB : t * SUB + stencil])
    acc[...] = jnp.zeros_like(acc)

    def one_point(k, _):
        value = u_ref[...] * full[pl.ds(k, 1), :]
        terms = two_terms(value).astype(BF16)
        acc[...] += scatter_product(terms, dep_ref[pl.ds(k, 1), :], cells)
        return 0

    lax.fori_loop(0, stencil, one_point, 0)
    for h in range(cells // LO):
        at = h * 2 * rows
        out_ref[:, h * LO : (h + 1) * LO] = acc[at : at + rows] + acc[at + rows : at + 2 * rows]


def arrive_kernel(local_ref, *refs):
    received, out_ref = refs[:-1], refs[-1]
    rows, cells = local_ref.shape
    values = jnp.concatenate([r[:rows, :] for r in received], axis=1)
    ids = jnp.concatenate([r[rows : rows + 1, :] for r in received], axis=1).astype(I32)
    sums = scatter_product(two_terms(values).astype(BF16), ids, cells)
    for h in range(cells // LO):
        at = h * 2 * rows
        span = slice(h * LO, (h + 1) * LO)
        out_ref[:, span] = local_ref[:, span] + (sums[at : at + rows] + sums[at + rows : at + 2 * rows])


def shifted(value, axis, distance):
    devices = range(lax.axis_size(axis))
    return lax.ppermute(value, axis, [(i - distance, i) for i in devices if i - distance in devices])


def rotated(value, axis, steps):
    count = lax.axis_size(axis)
    return lax.ppermute(value, axis, [(i, (i + steps) % count) for i in range(count)])


def body(adjoint_new, weights, departure, send_point, block_count, rotation):
    fields, levels, cells = adjoint_new.shape
    blocks, slots = send_point.shape
    stencil = departure.shape[0]
    rows = fields * levels
    count = lax.axis_size("lev")
    u = adjoint_new.reshape(rows, cells)
    bc = block_count.reshape(-1)
    rot = rotation.reshape(-1)
    parts = [weights] + [rotated(weights, "lev", s) for s in range(1, count)]
    full = pltpu.VMEM((stencil, cells), F32)
    block = jax.ShapeDtypeStruct((rows + SUB, slots), F32)
    outgoing = pl.pallas_call(
        lambda *refs: pick_kernel(count, levels, *refs),
        out_shape=[block] * blocks,
        in_specs=[VMEM, VMEM, VMEM, SMEM, SMEM] + [VMEM] * count,
        out_specs=[VMEM] * blocks,
        scratch_shapes=[full],
        cost_estimate=pl.CostEstimate(
            flops=4 * rows * cells * blocks * slots, bytes_accessed=4 * rows * cells, transcendentals=0
        ),
        compiler_params=PARAMS,
        name="pick",
    )(u, departure, send_point, bc, rot, *parts)
    received = [
        shifted(outgoing[1], "tile", 1),
        shifted(outgoing[0], "tile", -1),
        rotated(outgoing[3], "panel", 1),
        rotated(outgoing[2], "panel", -1),
    ]
    result = jax.ShapeDtypeStruct((rows, cells), F32)
    local = pl.pallas_call(
        lambda *refs: local_kernel(count, *refs),
        out_shape=result,
        in_specs=[VMEM, VMEM, VMEM, SMEM] + [VMEM] * count,
        out_specs=VMEM,
        scratch_shapes=[full, pltpu.VMEM((cells // LO * 2 * rows, LO), F32)],
        cost_estimate=pl.CostEstimate(
            flops=4 * rows * cells * stencil * cells, bytes_accessed=8 * rows * cells, transcendentals=0
        ),
        compiler_params=PARAMS,
        name="local",
    )(u, departure, send_point, bc, *parts)
    out = pl.pallas_call(
        arrive_kernel,
        out_shape=result,
        in_specs=[VMEM] * (1 + blocks),
        out_specs=VMEM,
        compiler_params=PARAMS,
        name="arrive",
    )(local, *received)
    return out.reshape(fields, levels, cells)


def solution(mesh):
    return jax.shard_map(
        body,
        mesh=mesh,
        in_specs=(
            P(None, "lev", ("panel", "tile")),
            P(None, ("panel", "tile", "lev")),
            P(None, ("panel", "tile")),
            P(None, ("panel", "tile")),
            P(None, ("panel", "tile")),
            P(None, ("panel", "tile")),
        ),
        out_specs=P(None, "lev", ("panel", "tile")),
        check_vma=False,
    )
```

time: 90.9 us -> 22.2 us (0.24)
  other arithmetic: 51.4 us -> 0 us
  local copies, waits for them, and re-layouts: 17.6 us -> 3.13 us
  Pallas kernels: 0 us -> 6.71 us
  blocking collectives: 5.33 us -> 0 us
  starting transfers between devices: 12.2 us -> 10.1 us
  waiting for transfers between devices: 3 us -> 1.94 us
    scatter-add x2 -> x0, other arithmetic: 48.4 us -> none  [the longest x1 44.6 us: body(): result = jnp.zeros((row_count, cell_count), jnp.float32).at[:, departure....]
    pallas_call x0 -> x3, Pallas kernels: none -> 6.71 us  [the longest x1 4.39 us: body(): pl.pallas_call(lambda *refs: local_kernel(count, *refs), out_shape=result...]
    gather x3 -> x0, local copies, waits for them, and re-layouts: 6.47 us -> none  [the longest x2 3.32 us: body(): weighted[:, chosen].reshape(fields, levels, blocks, slot_count)]
    mul x2 -> x0, local copies, waits for them, and re-layouts: 6.33 us -> none  [the longest x1 3.66 us: body(): adjoint_new[:, :, None, :] * weight_full[None, None, :, :]]
    all_gather x1 -> x0, blocking collectives: 5.33 us -> none  [body(): weight_full = lax.all_gather(weights, 'lev', axis=1, tiled=True)]
    scatter x1 -> x0, local copies, waits for them, and re-layouts: 2.48 us -> none  [body(): jnp.ones((points,), jnp.float32).at[dropped].set(0.0, mode='drop')]
    ppermute x8 -> x5, starting transfers between devices: 12.2 us -> 10.1 us  [the longest x2 5.31 us: shifted(): lax.ppermute(value, axis, [(i - distance, i) for i in devices if i - dist...]
    unnamed x15 -> x12, local copies, waits for them, and re-layouts: 1.16 us -> 3.13 us
  transfers between devices with their start and end apart: 8 -> 5, of which waited for: 1 -> 1; matrix products, arithmetic and copies ran while one was open for 56% -> 0% of each run, Pallas kernels for 0% -> 20%
where the time goes in v1:
time: 22.2 us; the launch traced here: 21.9 us
  starting transfers between devices  10.1 us (45%)
  Pallas kernels  6.71 us (30%)
  local copies, waits for them, and re-layouts  3.13 us (14%)
  waiting for transfers between devices  1.94 us (9%)
    ppermute x2, starting transfers between devices, shifted(): lax.ppermute(value, axis, [(i - distance, i) for i in devices if i - dist...  5.31 us
    ppermute x3, starting transfers between devices, rotated(): lax.ppermute(value, axis, [(i, (i + steps) % count) for i in range(count)])  4.76 us
    pallas_call x1, Pallas kernels, body(): pl.pallas_call(lambda *refs: local_kernel(count, *refs), out_shape=result...  4.39 us
    unnamed x12, local copies, waits for them, and re-layouts  3.13 us
    ppermute x3, waiting for transfers between devices, rotated(): lax.ppermute(value, axis, [(i, (i + steps) % count) for i in range(count)])  1.93 us
    pallas_call x1, Pallas kernels, body(): pl.pallas_call(lambda *refs: pick_kernel(count, levels, *refs), out_shape...  1.18 us
    pallas_call x1, Pallas kernels, body(): pl.pallas_call(arrive_kernel, out_shape=result, in_specs=[VMEM] * (1 + bl...  1.14 us
  transfers between devices with their start and end apart: 5, of which 1 were waited for; matrix products, arithmetic and copies ran while one was open for 0% of the time, Pallas kernels for 20%

profile of v1, /device:TPU:0, one launch (start us, length us, event | category | flops | bytes accessed | tf_op | source)
XLA Modules:
  0.0 21.9 jit_solution(11789222425125804885)
XLA Ops:
  0.0 3.0 %collective-permute-start = (f32[4,1024]{1,0:T(4,128)}, f32[4,1024]{1,0:T(4,128)S(1)}, u32[]{:S(2)}, u32[]{:S(2)}) collective-permute-start(f32[4,1024]{1,0:T(4,128)} %refs_5_.1), channel_id=1, source_target_pairs={{0,1},{1,0},{2,3},{3,2},{4,5},{5,4},{6,7},{7,6},{8,9},{9,8},{10,11... | collective-permute-start | bytes 49160 | tf_op jit(solution)/shard_map/ppermute | solution.py:165
  3.0 1.9 %collective-permute-done.refs_5_.refs_6_ = f32[4,1024]{1,0:T(4,128)S(1)} collective-permute-done((f32[4,1024]{1,0:T(4,128)}, f32[4,1024]{1,0:T(4,128)S(1)}, u32[]{:S(2)}, u32[]{:S(2)}) %collective-permute-start) | collective-permute-done | bytes 16416 | tf_op jit(solution)/shard_map/ppermute | solution.py:165
  4.9 0.0 copy-start.3
  4.9 0.0 copy-start.4
  4.9 0.0 copy-start.5
  4.9 0.7 %copy-done.3 = s32[4,128]{1,0:T(4,128)S(1)} copy-done((s32[4,128]{1,0:T(4,128)S(1)}, s32[4,128]{1,0:T(4,128)}, u32[]{:S(2)}) %copy-start.3) | copy-done | bytes 2072
  5.6 0.0 copy-done.4
  5.6 0.0 copy-done.5
  5.6 0.0 copy-start
  5.6 1.0 %copy-done = f32[5,8,2048]{2,1,0:T(8,128)S(1)} copy-done((f32[5,8,2048]{2,1,0:T(8,128)S(1)}, f32[5,8,2048]{2,1,0:T(8,128)}, u32[]{:S(2)}) %copy-start) | copy-done | bytes 327704
  6.6 0.0 copy-start.1
  6.6 0.8 %copy-done.1 = s32[4,2048]{1,0:T(4,128)S(1)} copy-done((s32[4,2048]{1,0:T(4,128)S(1)}, s32[4,2048]{1,0:T(4,128)}, u32[]{:S(2)}) %copy-start.1) | copy-done | bytes 32792
  7.3 0.0 copy-start.2
  7.3 0.7 %copy-done.2 = f32[4,1024]{1,0:T(4,128)S(1)} copy-done((f32[4,1024]{1,0:T(4,128)S(1)}, f32[4,1024]{1,0:T(4,128)}, u32[]{:S(2)}) %copy-start.2) | copy-done | bytes 16408
  8.0 1.2 %pick.1 = (f32[48,128]{1,0:T(8,128)S(1)}, f32[48,128]{1,0:T(8,128)S(1)}, f32[48,128]{1,0:T(8,128)S(1)}, f32[48,128]{1,0:T(8,128)S(1)}) custom-call(f32[40,2048]{1,0:T(8,128)S(1)} %bitcast.4, s32[4,2048]{1,0:T(4,128)S(1)} %copy-done.1, s32[4,128]{1,0:T(4,128)S(1)} %copy-done.3, s32[4]{0:T(128)S(1)} %bitcast.7, s32[2]{0:T(128)S(1)} %bitcast.6, ...), custom_call_target="tpu_custom_call" | custom-call | flops 167772160 | bytes 327680 | tf_op jit(solution)/shard_map/pick/pallas_call | solution.py:180
  9.2 4.0 %collective-permute-start.1 = (f32[48,128]{1,0:T(8,128)S(1)}, f32[48,128]{1,0:T(8,128)S(1)}, u32[]{:S(2)}, u32[]{:S(2)}) collective-permute-start(f32[48,128]{1,0:T(8,128)S(1)} %get-tuple-element.9), channel_id=1, source_target_pairs={{0,2},{2,4},{4,6},{1,3},{3,5},{5,7},{8,10},{10,12},{12,14},{9,11},... | collective-permute-start | bytes 73736 | tf_op jit(solution)/shard_map/ppermute | solution.py:160
  13.2 1.3 %collective-permute-start.2 = (f32[48,128]{1,0:T(8,128)S(1)}, f32[48,128]{1,0:T(8,128)S(1)}, u32[]{:S(2)}, u32[]{:S(2)}) collective-permute-start(f32[48,128]{1,0:T(8,128)S(1)} %get-tuple-element.10), channel_id=1, source_target_pairs={{2,0},{4,2},{6,4},{3,1},{5,3},{7,5},{10,8},{12,10},{14,12},{11,9},... | collective-permute-start | bytes 73736 | tf_op jit(solution)/shard_map/ppermute | solution.py:160
  14.5 0.1 collective-permute-start.3
  14.6 1.7 %collective-permute-start.4 = (f32[48,128]{1,0:T(8,128)S(1)}, f32[48,128]{1,0:T(8,128)S(1)}, u32[]{:S(2)}, u32[]{:S(2)}) collective-permute-start(f32[48,128]{1,0:T(8,128)S(1)} %get-tuple-element.12), channel_id=1, source_target_pairs={{0,24},{8,0},{16,8},{24,16},{1,25},{9,1},{17,9},{25,17},{2,26},{10... | collective-permute-start | bytes 73736 | tf_op jit(solution)/shard_map/ppermute | solution.py:165
  16.3 4.4 %local.1.local_ref = f32[40,2048]{1,0:T(8,128)S(1)} custom-call(f32[40,2048]{1,0:T(8,128)S(1)} %bitcast.5, s32[4,2048]{1,0:T(4,128)S(1)} %copy-done.1, s32[4,128]{1,0:T(4,128)S(1)} %copy-done.3, s32[4]{0:T(128)S(1)} %bitcast.8, f32[4,1024]{1,0:T(4,128)S(1)} %copy-done.2, f32[4,1024]{1,0:T(4,128)S(1)} %collective-permute-done.refs_5_.refs_6_), custom_call_target="tpu_custom_call" | custom-call | flops 2684354560 | bytes 655360 | tf_op jit(solution)/shard_map/local/pallas_call | solution.py:199
  20.7 0.0 collective-permute-done.1.refs_0_
  20.8 0.0 collective-permute-done.2.refs_1_
  20.8 0.0 collective-permute-done.3.refs_2_
  20.8 0.0 collective-permute-done.4.refs_3_
  20.8 1.1 %arrive.1 = f32[40,2048]{1,0:T(8,128)} custom-call(f32[40,2048]{1,0:T(8,128)S(1)} %local.1.local_ref, f32[48,128]{1,0:T(8,128)S(1)} %collective-permute-done.1.refs_0_, f32[48,128]{1,0:T(8,128)S(1)} %collective-permute-done.2.refs_1_, f32[48,128]{1,0:T(8,128)S(1)} %collective-permute-done.3.refs_2_, f32[48,128]{1,0:T(8,128)S(1)} %collective-permute-done.4.refs_3_), custom_call_target="tpu_custom_call" | custom-call | tf_op jit(solution)/shard_map/arrive/pallas_call | solution.py:211
Async XLA Ops:
  0.0 4.9 %collective-permute-start = (f32[4,1024]{1,0:T(4,128)}, f32[4,1024]{1,0:T(4,128)S(1)}, u32[]{:S(2)}, u32[]{:S(2)}) collective-permute-start(f32[4,1024]{1,0:T(4,128)} %refs_5_.1), channel_id=1, source_target_pairs={{0,1},{1,0},{2,3},{3,2},{4,5},{5,4},{6,7},{7,6},{8,9},{9,8},{10,11... | collective-permute-start | bytes 49160 | tf_op jit(solution)/shard_map/ppermute | solution.py:165
  4.9 0.7 %copy-start.3 = (s32[4,128]{1,0:T(4,128)S(1)}, s32[4,128]{1,0:T(4,128)}, u32[]{:S(2)}) copy-start(s32[4,128]{1,0:T(4,128)} %refs_2_.3) | copy-start | bytes 6148
  4.9 0.7 %copy-start.4 = (s32[2,1]{0,1:T(1,128)S(1)}, s32[2,1]{0,1:T(1,128)}, u32[]{:S(2)}) copy-start(s32[2,1]{0,1:T(1,128)} %param.11) | copy-start | bytes 28
  4.9 0.7 %copy-start.5 = (s32[4,1]{0,1:T(1,128)S(1)}, s32[4,1]{0,1:T(1,128)}, u32[]{:S(2)}) copy-start(s32[4,1]{0,1:T(1,128)} %param.10) | copy-start | bytes 52
  5.6 1.0 %copy-start = (f32[5,8,2048]{2,1,0:T(8,128)S(1)}, f32[5,8,2048]{2,1,0:T(8,128)}, u32[]{:S(2)}) copy-start(f32[5,8,2048]{2,1,0:T(8,128)} %param.6) | copy-start | bytes 983044
  6.6 0.8 %copy-start.1 = (s32[4,2048]{1,0:T(4,128)S(1)}, s32[4,2048]{1,0:T(4,128)}, u32[]{:S(2)}) copy-start(s32[4,2048]{1,0:T(4,128)} %refs_1_.3) | copy-start | bytes 98308
  7.3 0.7 %copy-start.2 = (f32[4,1024]{1,0:T(4,128)S(1)}, f32[4,1024]{1,0:T(4,128)}, u32[]{:S(2)}) copy-start(f32[4,1024]{1,0:T(4,128)} %refs_5_.1) | copy-start | bytes 49156
  9.2 11.5 %collective-permute-start.1 = (f32[48,128]{1,0:T(8,128)S(1)}, f32[48,128]{1,0:T(8,128)S(1)}, u32[]{:S(2)}, u32[]{:S(2)}) collective-permute-start(f32[48,128]{1,0:T(8,128)S(1)} %get-tuple-element.9), channel_id=1, source_target_pairs={{0,2},{2,4},{4,6},{1,3},{3,5},{5,7},{8,10},{10,12},{12,14},{9,11},... | collective-permute-start | bytes 73736 | tf_op jit(solution)/shard_map/ppermute | solution.py:160
  13.2 7.5 %collective-permute-start.2 = (f32[48,128]{1,0:T(8,128)S(1)}, f32[48,128]{1,0:T(8,128)S(1)}, u32[]{:S(2)}, u32[]{:S(2)}) collective-permute-start(f32[48,128]{1,0:T(8,128)S(1)} %get-tuple-element.10), channel_id=1, source_target_pairs={{2,0},{4,2},{6,4},{3,1},{5,3},{7,5},{10,8},{12,10},{14,12},{11,9},... | collective-permute-start | bytes 73736 | tf_op jit(solution)/shard_map/ppermute | solution.py:160
  14.5 6.2 %collective-permute-start.3 = (f32[48,128]{1,0:T(8,128)S(1)}, f32[48,128]{1,0:T(8,128)S(1)}, u32[]{:S(2)}, u32[]{:S(2)}) collective-permute-start(f32[48,128]{1,0:T(8,128)S(1)} %get-tuple-element.11), channel_id=1, source_target_pairs={{0,8},{8,16},{16,24},{24,0},{1,9},{9,17},{17,25},{25,1},{2,10},{10... | collective-permute-start | bytes 73736 | tf_op jit(solution)/shard_map/ppermute | solution.py:165
  14.6 6.2 %collective-permute-start.4 = (f32[48,128]{1,0:T(8,128)S(1)}, f32[48,128]{1,0:T(8,128)S(1)}, u32[]{:S(2)}, u32[]{:S(2)}) collective-permute-start(f32[48,128]{1,0:T(8,128)S(1)} %get-tuple-element.12), channel_id=1, source_target_pairs={{0,24},{8,0},{16,8},{24,16},{1,25},{9,1},{17,9},{25,17},{2,26},{10... | collective-permute-start | bytes 73736 | tf_op jit(solution)/shard_map/ppermute | solution.py:165

commit v2 on v0

v2 whole, which is shorter than its diff:
```python
import jax
import jax.numpy as jnp
from jax import lax
from jax.experimental import pallas as pl
from jax.experimental.pallas import tpu as pltpu
from jax.sharding import PartitionSpec as P

F32, BF16, I32 = jnp.float32, jnp.bfloat16, jnp.int32
LO = 256
LANES = 128
SUB = 8
VMEM = pl.BlockSpec(memory_space=pltpu.VMEM)
HBM = pl.BlockSpec(memory_space=pltpu.HBM)
PARAMS = pltpu.CompilerParams(vmem_limit_bytes=32 << 20)
NT = (((1,), (1,)), ((), ()))


def one_hot(rows, index):
    row = lax.broadcasted_iota(I32, (rows, index.shape[1]), 0)
    return (row == index).astype(F32).astype(BF16)


def two_terms(value):
    high = value.astype(BF16).astype(F32)
    return jnp.concatenate([high, value - high], axis=0)


def scatter_product(terms, target, cells):
    high = target // LO
    low = target - high * LO
    left = jnp.concatenate(
        [terms * (high == h).astype(F32).astype(BF16) for h in range(cells // LO)], axis=0
    )
    return lax.dot_general(left, one_hot(LO, low), NT, preferred_element_type=F32)


def prepare_kernel(
    levels, u_hbm, w_hbm, dep_hbm, sp_hbm, bc_hbm, rot_hbm,
    u_ref, w_ref, dep_ref, keep_ref, picked_ref, live_ref, lane_ref,
    sp_ref, bc_ref, rot_ref, sems,
):
    pairs = [(sp_hbm, sp_ref), (bc_hbm, bc_ref), (rot_hbm, rot_ref), (dep_hbm, dep_ref), (u_hbm, u_ref), (w_hbm, w_ref)]
    copies = [pltpu.make_async_copy(a, b, sems.at[i]) for i, (a, b) in enumerate(pairs)]
    for c in copies:
        c.start()
    for c in copies[:3]:
        c.wait()
    rows, cells = u_ref.shape
    stencil = dep_ref.shape[0]
    blocks, slots = sp_ref.shape
    tiles = cells // LANES
    slot = lax.broadcasted_iota(I32, (1, slots), 1)
    which, columns, codes, lanes = [], [], [], []
    for j in range(blocks):
        chosen = sp_ref[j : j + 1, :]
        k = chosen // cells
        column = chosen - k * cells
        tile = column // LANES
        which.append(k)
        columns.append(column)
        codes.append(jnp.where(slot < bc_ref[0:1, j : j + 1], tile * SUB + k, -1))
        lanes.append(column - tile * LANES)
    live = one_hot(tiles * SUB, jnp.concatenate(codes, axis=1))
    lane = one_hot(LANES, jnp.concatenate(lanes, axis=1))
    live_ref[...] = live
    lane_ref[...] = lane
    sent = lax.dot_general(live, lane, NT, preferred_element_type=F32)
    for t in range(tiles):
        keep_ref[:, t * LANES : (t + 1) * LANES] = 1.0 - sent[t * SUB : t * SUB + stencil]
    onehot = one_hot(cells, jnp.concatenate(columns, axis=1))
    for c in copies[3:]:
        c.wait()
    dep = dep_ref[...]
    dep_high = dep // SUB
    dep_low = dep - dep_high * SUB
    table = jnp.concatenate(
        [two_terms(u_ref[...]), jnp.concatenate([dep_high.astype(F32), dep_low.astype(F32)], axis=0), jnp.zeros((SUB, cells), F32)],
        axis=0,
    ).astype(BF16)
    got = jnp.dot(table, onehot, preferred_element_type=F32)
    at = 2 * rows
    for j in range(blocks):
        here = slice(j * slots, (j + 1) * slots)
        g = got[:, here]
        ids = jnp.zeros((1, slots), F32)
        for k in range(stencil):
            one_id = g[at + k : at + k + 1] * SUB + g[at + stencil + k : at + stencil + k + 1]
            ids = ids + jnp.where(which[j] == k, one_id, 0.0)
        values = g[:rows] + g[rows : 2 * rows]
        zonal, merid = values[:levels], values[levels : 2 * levels]
        if j >= 2:
            code = rot_ref[0:1, j - 2 : j - 1]
            cosine = (code == 0).astype(F32) - (code == 2).astype(F32)
            sine = (code == 1).astype(F32) - (code == 3).astype(F32)
            zonal, merid = cosine * zonal + sine * merid, cosine * merid - sine * zonal
        picked_ref[:levels, here] = zonal
        picked_ref[levels : 2 * levels, here] = merid
        picked_ref[2 * levels : rows, here] = values[2 * levels :]
        picked_ref[rows:, here] = jnp.broadcast_to(ids, (SUB, slots))


def place_weights(parts, full):
    count = len(parts)
    width = parts[0].shape[1]
    me = lax.axis_index("lev")
    for s, part in enumerate(parts):
        source = lax.rem(me + (count - s), count)
        full[:, pl.ds(pl.multiple_of(source * width, LANES), width)] = part[...]


def send_kernel(count, paired, picked_ref, live_ref, lane_ref, keep_ref, *refs):
    parts, outs, masked_ref, full = refs[:count], refs[count:-2], refs[-2], refs[-1]
    stencil, cells = full.shape
    rows = picked_ref.shape[0] - SUB
    blocks, slots = len(outs), outs[0].shape[1]
    place_weights(parts, full)
    pad = jnp.zeros((SUB - stencil, LANES), F32)
    pieces = []
    for t in range(cells // LANES):
        pieces += [full[:, t * LANES : (t + 1) * LANES], pad]
    w = jnp.concatenate(pieces, axis=0)
    w0 = w.astype(BF16).astype(F32)
    w1 = (w - w0).astype(BF16).astype(F32)
    terms = jnp.concatenate([w0, w1, w - w0 - w1], axis=0).astype(BF16)
    got = jnp.dot(terms, lane_ref[...], preferred_element_type=F32)
    n = w.shape[0]
    got = (got[:n] + got[n : 2 * n] + got[2 * n :]) * live_ref[...].astype(F32)
    weight = jnp.sum(got, axis=0, keepdims=True)
    message = [
        jnp.concatenate(
            [picked_ref[:rows, j * slots : (j + 1) * slots] * weight[:, j * slots : (j + 1) * slots], picked_ref[rows:, j * slots : (j + 1) * slots]],
            axis=0,
        )
        for j in range(blocks)
    ]
    if paired:
        even = lax.rem(lax.axis_index("panel"), 2) == 0
        low, high, previous, following = message
        message = [
            jnp.where(even, high, low),
            jnp.where(even, low, high),
            jnp.where(even, following, previous),
            jnp.where(even, previous, following),
        ]
    for out, m in zip(outs, message):
        out[...] = m
    masked_ref[...] = full[...] * keep_ref[...]


def local_kernel(u_ref, dep_ref, w_ref, out_ref, acc):
    rows, cells = u_ref.shape
    stencil = dep_ref.shape[0]
    acc[...] = jnp.zeros_like(acc)

    def one_point(k, _):
        value = u_ref[...] * w_ref[pl.ds(k, 1), :]
        terms = two_terms(value).astype(BF16)
        acc[...] += scatter_product(terms, dep_ref[pl.ds(k, 1), :], cells)
        return 0

    lax.fori_loop(0, stencil, one_point, 0)
    for h in range(cells // LO):
        at = h * 2 * rows
        out_ref[:, h * LO : (h + 1) * LO] = acc[at : at + rows] + acc[at + rows : at + 2 * rows]


def arrive_kernel(local_ref, *refs):
    received, out_ref = refs[:-1], refs[-1]
    rows, cells = local_ref.shape
    values = jnp.concatenate([r[:rows, :] for r in received], axis=1)
    ids = jnp.concatenate([r[rows : rows + 1, :] for r in received], axis=1).astype(I32)
    sums = scatter_product(two_terms(values).astype(BF16), ids, cells)
    for h in range(cells // LO):
        at = h * 2 * rows
        span = slice(h * LO, (h + 1) * LO)
        out_ref[:, span] = local_ref[:, span] + (sums[at : at + rows] + sums[at + rows : at + 2 * rows])


def rotated(value, axis, steps):
    count = lax.axis_size(axis)
    return lax.ppermute(value, axis, [(i, (i + steps) % count) for i in range(count)])


def racetrack(value, reverse):
    sectors, tiles = lax.axis_size("panel"), lax.axis_size("tile")
    route = []
    for p in range(sectors):
        step = 1 if (p % 2 == 0) != reverse else -1
        for t in range(tiles):
            q, to = (p, t + step) if 0 <= t + step < tiles else (p ^ 1, t)
            route.append((p * tiles + t, q * tiles + to))
    return lax.ppermute(value, ("panel", "tile"), route)


def swapped(value, outer):
    count = lax.axis_size("panel")
    step = [1, -1] if not outer else [-1, 1]
    return lax.ppermute(value, "panel", [(i, (i + step[i % 2]) % count) for i in range(count)])


def body(adjoint_new, weights, departure, send_point, block_count, rotation):
    fields, levels, cells = adjoint_new.shape
    blocks, slots = send_point.shape
    stencil = departure.shape[0]
    rows = fields * levels
    count = lax.axis_size("lev")
    paired = lax.axis_size("panel") % 2 == 0
    points = blocks * slots
    shape = jax.ShapeDtypeStruct
    parts = [rotated(weights, "lev", s) for s in range(1, count)]
    inputs = (
        adjoint_new.reshape(rows, cells), weights, departure, send_point,
        block_count.reshape(1, -1), rotation.reshape(1, -1),
    )
    u, own, dep, keep, picked, live, lane = pl.pallas_call(
        lambda *refs: prepare_kernel(levels, *refs),
        out_shape=[
            shape((rows, cells), F32),
            shape(weights.shape, F32),
            shape((stencil, cells), I32),
            shape((stencil, cells), F32),
            shape((rows + SUB, points), F32),
            shape((cells // LANES * SUB, points), BF16),
            shape((LANES, points), BF16),
        ],
        in_specs=[HBM] * 6,
        out_specs=[VMEM] * 7,
        scratch_shapes=[
            pltpu.VMEM((blocks, slots), I32),
            pltpu.VMEM((1, block_count.size), I32),
            pltpu.VMEM((1, rotation.size), I32),
            pltpu.SemaphoreType.DMA((6,)),
        ],
        cost_estimate=pl.CostEstimate(
            flops=4 * rows * cells * points, bytes_accessed=8 * rows * cells, transcendentals=0
        ),
        compiler_params=PARAMS,
        name="prepare",
    )(*(pltpu.with_memory_space_constraint(a, pltpu.HBM) for a in inputs))
    block = shape((rows + SUB, slots), F32)
    *outgoing, masked = pl.pallas_call(
        lambda *refs: send_kernel(count, paired, *refs),
        out_shape=[block] * blocks + [shape((stencil, cells), F32)],
        in_specs=[VMEM] * (4 + count),
        out_specs=[VMEM] * (blocks + 1),
        scratch_shapes=[pltpu.VMEM((stencil, cells), F32)],
        compiler_params=PARAMS,
        name="send",
    )(picked, live, lane, keep, own, *parts)
    if paired:
        received = [
            racetrack(outgoing[0], False),
            racetrack(outgoing[1], True),
            swapped(outgoing[2], False),
            swapped(outgoing[3], True),
        ]
    else:
        received = [
            rotated(outgoing[1], "tile", 1),
            rotated(outgoing[0], "tile", -1),
            rotated(outgoing[3], "panel", 1),
            rotated(outgoing[2], "panel", -1),
        ]
    result = shape((rows, cells), F32)
    local = pl.pallas_call(
        local_kernel,
        out_shape=result,
        in_specs=[VMEM] * 3,
        out_specs=VMEM,
        scratch_shapes=[pltpu.VMEM((cells // LO * 2 * rows, LO), F32)],
        cost_estimate=pl.CostEstimate(
            flops=4 * rows * cells * stencil * cells, bytes_accessed=8 * rows * cells, transcendentals=0
        ),
        compiler_params=PARAMS,
        name="local",
    )(u, dep, masked)
    out = pl.pallas_call(
        arrive_kernel,
        out_shape=result,
        in_specs=[VMEM] * (1 + blocks),
        out_specs=VMEM,
        compiler_params=PARAMS,
        name="arrive",
    )(local, *received)
    return out.reshape(fields, levels, cells)


def solution(mesh):
    return jax.shard_map(
        body,
        mesh=mesh,
        in_specs=(
            P(None, "lev", ("panel", "tile")),
            P(None, ("panel", "tile", "lev")),
            P(None, ("panel", "tile")),
            P(None, ("panel", "tile")),
            P(None, ("panel", "tile")),
            P(None, ("panel", "tile")),
        ),
        out_specs=P(None, "lev", ("panel", "tile")),
        check_vma=False,
    )
```

time: 90.9 us -> 13.9 us (0.15); the launches traced: 89.8 us -> 13.8 us
  other arithmetic: 51.4 us -> 0 us
  local copies, waits for them, and re-layouts: 17.6 us -> 0 us
  Pallas kernels: 0 us -> 7.05 us
  starting transfers between devices: 12.2 us -> 6.64 us
  blocking collectives: 5.33 us -> 0 us
  waiting for transfers between devices: 3 us -> 0.01 us
    scatter-add x2 -> x0, other arithmetic: 48.4 us -> none  [the longest x1 44.6 us: body(): result = jnp.zeros((row_count, cell_count), jnp.float32).at[:, departure....]
    pallas_call x0 -> x4, Pallas kernels: none -> 7.05 us  [the longest x1 3.65 us: body(): pl.pallas_call(local_kernel, out_shape=result, in_specs=[VMEM] * 3, out_s...]
    gather x3 -> x0, local copies, waits for them, and re-layouts: 6.47 us -> none  [the longest x2 3.32 us: body(): weighted[:, chosen].reshape(fields, levels, blocks, slot_count)]
    mul x2 -> x0, local copies, waits for them, and re-layouts: 6.33 us -> none  [the longest x1 3.66 us: body(): adjoint_new[:, :, None, :] * weight_full[None, None, :, :]]
    ppermute x8 -> x5, starting transfers between devices: 12.2 us -> 6.64 us  [the longest x1 2.97 us: rotated(): lax.ppermute(value, axis, [(i, (i + steps) % count) for i in range(count)])]
    all_gather x1 -> x0, blocking collectives: 5.33 us -> none  [body(): weight_full = lax.all_gather(weights, 'lev', axis=1, tiled=True)]
    ppermute x8 -> x5, waiting for transfers between devices: 3 us -> 0.01 us  [the longest x2 0.01 us: racetrack(): return lax.ppermute(value, ('panel', 'tile'), route)]
    scatter x1 -> x0, local copies, waits for them, and re-layouts: 2.48 us -> none  [body(): jnp.ones((points,), jnp.float32).at[dropped].set(0.0, mode='drop')]
  transfers between devices with their start and end apart: 8 -> 5, of which waited for: 1 -> 0; matrix products, arithmetic and copies ran while one was open for 56% -> 0% of each run, Pallas kernels for 0% -> 41%
where the time goes in v2:
time: 13.9 us; the launch traced here: 13.8 us
  Pallas kernels  7.05 us (51%)
  starting transfers between devices  6.64 us (48%)
    pallas_call x1, Pallas kernels, body(): pl.pallas_call(local_kernel, out_shape=result, in_specs=[VMEM] * 3, out_s...  3.65 us
    ppermute x1, starting transfers between devices, rotated(): lax.ppermute(value, axis, [(i, (i + steps) % count) for i in range(count)])  2.97 us
    ppermute x2, starting transfers between devices, racetrack(): return lax.ppermute(value, ('panel', 'tile'), route)  2.04 us
    pallas_call x1, Pallas kernels, body(): pl.pallas_call(lambda *refs: prepare_kernel(levels, *refs), out_shape=[sh...  2 us
    ppermute x2, starting transfers between devices, swapped(): lax.ppermute(value, 'panel', [(i, (i + step[i % 2]) % count) for i in ran...  1.63 us
    pallas_call x1, Pallas kernels, body(): pl.pallas_call(arrive_kernel, out_shape=result, in_specs=[VMEM] * (1 + bl...  1.14 us
  transfers between devices with their start and end apart: 5, of which 0 were waited for; matrix products, arithmetic and copies ran while one was open for 0% of the time, Pallas kernels for 41%

profile of v2, /device:TPU:0, one launch (start us, length us, event | category | flops | bytes accessed | tf_op | source)
XLA Modules:
  0.0 13.8 jit_solution(7182086568714530810)
XLA Ops:
  0.0 3.0 %collective-permute-start = (f32[4,1024]{1,0:T(4,128)}, f32[4,1024]{1,0:T(4,128)S(1)}, u32[]{:S(2)}, u32[]{:S(2)}) collective-permute-start(f32[4,1024]{1,0:T(4,128)} %refs_1_.1), channel_id=1, source_target_pairs={{0,1},{1,0},{2,3},{3,2},{4,5},{5,4},{6,7},{7,6},{8,9},{9,8},{10,11... | collective-permute-start | bytes 49160 | tf_op jit(solution)/shard_map/ppermute | solution.py:181
  3.0 2.0 %prepare.1 = (f32[40,2048]{1,0:T(8,128)S(1)}, f32[4,1024]{1,0:T(4,128)S(1)}, s32[4,2048]{1,0:T(4,128)S(1)}, f32[4,2048]{1,0:T(4,128)S(1)}, f32[48,512]{1,0:T(8,1...) custom-call(f32[40,2048]{1,0:T(8,128)} %bitcast.4, f32[4,1024]{1,0:T(4,128)} %refs_1_.1, ...), custom_call_target="tpu_custom_call" | custom-call | flops 167772160 | bytes 655360 | tf_op jit(solution)/shard_map/prepare/pallas_call | solution.py:215
  5.0 0.0 collective-permute-done.refs_5_
  5.0 0.3 %send.1 = (f32[48,128]{1,0:T(8,128)S(1)}, f32[48,128]{1,0:T(8,128)S(1)}, f32[48,128]{1,0:T(8,128)S(1)}, f32[48,128]{1,0:T(8,128)S(1)}, f32[4,2048]{1,0:T(4,128)S(1)}) custom-call(f32[48,512]{1,0:T(8,128)S(1)} %get-tuple-element.19.refs_0_, bf16[128,512]{1,0:T(8,128)(2,1)S(1)} %get-tuple-element.20.refs_1_, bf16[128,512]{1,0:T(8,128)(2,1)S(1)} %get-tuple-element.21.refs_2_, ...), custom_call_target="tpu_custom_call" | custom-call | tf_op jit(solution)/shard_map/send/pallas_call | solution.py:241
  5.3 2.0 %collective-permute-start.1 = (f32[48,128]{1,0:T(8,128)S(1)}, f32[48,128]{1,0:T(8,128)S(1)}, u32[]{:S(2)}, u32[]{:S(2)}) collective-permute-start(f32[48,128]{1,0:T(8,128)S(1)} %get-tuple-element.25), channel_id=1, source_target_pairs={{0,2},{2,4},{4,6},{6,14},{8,0},{10,8},{12,10},{14,12},{16,18},{18,... | collective-permute-start | bytes 73736 | tf_op jit(solution)/shard_map/ppermute | solution.py:192
  7.3 0.0 collective-permute-start.2
  7.3 0.0 collective-permute-start.3
  7.3 1.6 %collective-permute-start.4 = (f32[48,128]{1,0:T(8,128)S(1)}, f32[48,128]{1,0:T(8,128)S(1)}, u32[]{:S(2)}, u32[]{:S(2)}) collective-permute-start(f32[48,128]{1,0:T(8,128)S(1)} %get-tuple-element.28), channel_id=1, source_target_pairs={{0,24},{8,16},{16,8},{24,0},{1,25},{9,17},{17,9},{25,1},{2,26},{10... | collective-permute-start | bytes 73736 | tf_op jit(solution)/shard_map/ppermute | solution.py:198
  8.9 3.6 %local.1.local_ref = f32[40,2048]{1,0:T(8,128)S(1)} custom-call(f32[40,2048]{1,0:T(8,128)S(1)} %get-tuple-element.17.u_ref, s32[4,2048]{1,0:T(4,128)S(1)} %get-tuple-element.18.dep_ref, f32[4,2048]{1,0:T(4,128)S(1)} %get-tuple-element.24.w_ref), custom_call_target="tpu_custom_call" | custom-call | flops 2684354560 | bytes 655360 | tf_op jit(solution)/shard_map/local/pallas_call | solution.py:265
  12.6 0.0 collective-permute-done.1.refs_0_
  12.6 0.0 collective-permute-done.2.refs_1_
  12.6 0.0 collective-permute-done.3.refs_2_
  12.6 0.0 collective-permute-done.4.refs_3_
  12.6 1.1 %arrive.1 = f32[40,2048]{1,0:T(8,128)} custom-call(f32[40,2048]{1,0:T(8,128)S(1)} %local.1.local_ref, f32[48,128]{1,0:T(8,128)S(1)} %collective-permute-done.1.refs_0_, f32[48,128]{1,0:T(8,128)S(1)} %collective-permute-done.2.refs_1_, f32[48,128]{1,0:T(8,128)S(1)} %collective-permute-done.3.refs_2_, f32[48,128]{1,0:T(8,128)S(1)} %collective-permute-done.4.refs_3_), custom_call_target="tpu_custom_call" | custom-call | tf_op jit(solution)/shard_map/arrive/pallas_call | solution.py:277
Async XLA Ops:
  0.0 5.0 %collective-permute-start = (f32[4,1024]{1,0:T(4,128)}, f32[4,1024]{1,0:T(4,128)S(1)}, u32[]{:S(2)}, u32[]{:S(2)}) collective-permute-start(f32[4,1024]{1,0:T(4,128)} %refs_1_.1), channel_id=1, source_target_pairs={{0,1},{1,0},{2,3},{3,2},{4,5},{5,4},{6,7},{7,6},{8,9},{9,8},{10,11... | collective-permute-start | bytes 49160 | tf_op jit(solution)/shard_map/ppermute | solution.py:181
  5.3 7.3 %collective-permute-start.1 = (f32[48,128]{1,0:T(8,128)S(1)}, f32[48,128]{1,0:T(8,128)S(1)}, u32[]{:S(2)}, u32[]{:S(2)}) collective-permute-start(f32[48,128]{1,0:T(8,128)S(1)} %get-tuple-element.25), channel_id=1, source_target_pairs={{0,2},{2,4},{4,6},{6,14},{8,0},{10,8},{12,10},{14,12},{16,18},{18,... | collective-permute-start | bytes 73736 | tf_op jit(solution)/shard_map/ppermute | solution.py:192
  7.3 5.3 %collective-permute-start.2 = (f32[48,128]{1,0:T(8,128)S(1)}, f32[48,128]{1,0:T(8,128)S(1)}, u32[]{:S(2)}, u32[]{:S(2)}) collective-permute-start(f32[48,128]{1,0:T(8,128)S(1)} %get-tuple-element.26), channel_id=1, source_target_pairs={{0,8},{2,0},{4,2},{6,4},{8,10},{10,12},{12,14},{14,6},{16,24},{18,... | collective-permute-start | bytes 73736 | tf_op jit(solution)/shard_map/ppermute | solution.py:192
  7.3 5.3 %collective-permute-start.3 = (f32[48,128]{1,0:T(8,128)S(1)}, f32[48,128]{1,0:T(8,128)S(1)}, u32[]{:S(2)}, u32[]{:S(2)}) collective-permute-start(f32[48,128]{1,0:T(8,128)S(1)} %get-tuple-element.27), channel_id=1, source_target_pairs={{0,8},{8,0},{16,24},{24,16},{1,9},{9,1},{17,25},{25,17},{2,10},{10... | collective-permute-start | bytes 73736 | tf_op jit(solution)/shard_map/ppermute | solution.py:198
  7.3 5.3 %collective-permute-start.4 = (f32[48,128]{1,0:T(8,128)S(1)}, f32[48,128]{1,0:T(8,128)S(1)}, u32[]{:S(2)}, u32[]{:S(2)}) collective-permute-start(f32[48,128]{1,0:T(8,128)S(1)} %get-tuple-element.28), channel_id=1, source_target_pairs={{0,24},{8,16},{16,8},{24,0},{1,25},{9,17},{17,9},{25,1},{2,26},{10... | collective-permute-start | bytes 73736 | tf_op jit(solution)/shard_map/ppermute | solution.py:198

commit v3 on v2

--- a/solution.py
+++ b/solution.py
@@ -25,13 +25,16 @@
     return jnp.concatenate([high, value - high], axis=0)
 
 
-def scatter_product(terms, target, cells):
-    high = target // LO
-    low = target - high * LO
-    left = jnp.concatenate(
-        [terms * (high == h).astype(F32).astype(BF16) for h in range(cells // LO)], axis=0
-    )
-    return lax.dot_general(left, one_hot(LO, low), NT, preferred_element_type=F32)
+def scatter_product(segments, cells):
+    left = [[] for _ in range(cells // LO)]
+    right = []
+    for terms, target in segments:
+        high = target // LO
+        for h, row in enumerate(left):
+            row.append(terms * (high == h).astype(F32).astype(BF16))
+        right.append(one_hot(LO, target - high * LO))
+    left = jnp.concatenate([jnp.concatenate(row, axis=1) for row in left], axis=0)
+    return lax.dot_general(left, jnp.concatenate(right, axis=1), NT, preferred_element_type=F32)
 
 
 def prepare_kernel(
@@ -147,33 +150,26 @@
     masked_ref[...] = full[...] * keep_ref[...]
 
 
-def local_kernel(u_ref, dep_ref, w_ref, out_ref, acc):
-    rows, cells = u_ref.shape
-    stencil = dep_ref.shape[0]
-    acc[...] = jnp.zeros_like(acc)
-
-    def one_point(k, _):
-        value = u_ref[...] * w_ref[pl.ds(k, 1), :]
-        terms = two_terms(value).astype(BF16)
-        acc[...] += scatter_product(terms, dep_ref[pl.ds(k, 1), :], cells)
-        return 0
-
-    lax.fori_loop(0, stencil, one_point, 0)
-    for h in range(cells // LO):
-        at = h * 2 * rows
-        out_ref[:, h * LO : (h + 1) * LO] = acc[at : at + rows] + acc[at + rows : at + 2 * rows]
-
-
-def arrive_kernel(local_ref, *refs):
+def local_kernel(u_ref, dep_ref, w_ref, acc_ref):
+    cells = u_ref.shape[1]
+    acc_ref[...] = scatter_product(
+        [
+            (two_terms(u_ref[...] * w_ref[k : k + 1, :]).astype(BF16), dep_ref[k : k + 1, :])
+            for k in range(dep_ref.shape[0])
+        ],
+        cells,
+    )
+
+
+def arrive_kernel(acc_ref, *refs):
     received, out_ref = refs[:-1], refs[-1]
-    rows, cells = local_ref.shape
+    rows, cells = out_ref.shape
     values = jnp.concatenate([r[:rows, :] for r in received], axis=1)
     ids = jnp.concatenate([r[rows : rows + 1, :] for r in received], axis=1).astype(I32)
-    sums = scatter_product(two_terms(values).astype(BF16), ids, cells)
+    sums = scatter_product([(two_terms(values).astype(BF16), ids)], cells)
     for h in range(cells // LO):
-        at = h * 2 * rows
-        span = slice(h * LO, (h + 1) * LO)
-        out_ref[:, span] = local_ref[:, span] + (sums[at : at + rows] + sums[at + rows : at + 2 * rows])
+        a, b, c = (2 * h * rows + i * rows for i in range(3))
+        out_ref[:, h * LO : (h + 1) * LO] = (acc_ref[a:b] + acc_ref[b:c]) + (sums[a:b] + sums[b:c])
 
 
 def rotated(value, axis, steps):
@@ -261,13 +257,11 @@
             rotated(outgoing[3], "panel", 1),
             rotated(outgoing[2], "panel", -1),
         ]
-    result = shape((rows, cells), F32)
     local = pl.pallas_call(
         local_kernel,
-        out_shape=result,
+        out_shape=shape((cells // LO * 2 * rows, LO), F32),
         in_specs=[VMEM] * 3,
         out_specs=VMEM,
-        scratch_shapes=[pltpu.VMEM((cells // LO * 2 * rows, LO), F32)],
         cost_estimate=pl.CostEstimate(
             flops=4 * rows * cells * stencil * cells, bytes_accessed=8 * rows * cells, transcendentals=0
         ),
@@ -276,7 +270,7 @@
     )(u, dep, masked)
     out = pl.pallas_call(
         arrive_kernel,
-        out_shape=result,
+        out_shape=shape((rows, cells), F32),
         in_specs=[VMEM] * (1 + blocks),
         out_specs=VMEM,
         compiler_params=PARAMS,

time: 13.9 us -> 13.2 us (0.950)
  Pallas kernels: 7.05 us -> 6.32 us
    pallas_call x2, Pallas kernels: 4.79 us -> 4.05 us  [the longest x1 2.91 us: body(): pl.pallas_call(local_kernel, out_shape=shape((cells // LO * 2 * rows, LO)...]
  transfers between devices with their start and end apart: 5 -> 5, of which waited for: 0 -> 0; matrix products, arithmetic and copies ran while one was open for 0% -> 0% of each run, Pallas kernels for 41% -> 38%
where the time goes in v3:
time: 13.2 us; the launch traced here: 13 us
  starting transfers between devices  6.64 us (50%)
  Pallas kernels  6.32 us (48%)
    ppermute x1, starting transfers between devices, rotated(): lax.ppermute(value, axis, [(i, (i + steps) % count) for i in range(count)])  2.97 us
    pallas_call x1, Pallas kernels, body(): pl.pallas_call(local_kernel, out_shape=shape((cells // LO * 2 * rows, LO)...  2.91 us
    ppermute x2, starting transfers between devices, racetrack(): return lax.ppermute(value, ('panel', 'tile'), route)  2.04 us
    pallas_call x1, Pallas kernels, body(): pl.pallas_call(lambda *refs: prepare_kernel(levels, *refs), out_shape=[sh...  2 us
    ppermute x2, starting transfers between devices, swapped(): lax.ppermute(value, 'panel', [(i, (i + step[i % 2]) % count) for i in ran...  1.63 us
    pallas_call x1, Pallas kernels, body(): pl.pallas_call(arrive_kernel, out_shape=shape((rows, cells), F32), in_spe...  1.14 us
    pallas_call x1, Pallas kernels, body(): pl.pallas_call(lambda *refs: send_kernel(count, paired, *refs), out_shape...  0.27 us
  transfers between devices with their start and end apart: 5, of which 0 were waited for; matrix products, arithmetic and copies ran while one was open for 0% of the time, Pallas kernels for 38%

profile of v3, /device:TPU:0, one launch (start us, length us, event | category | flops | bytes accessed | tf_op | source)
XLA Modules:
  0.0 13.0 jit_solution(18122605988102758412)
XLA Ops:
  0.0 3.0 %collective-permute-start = (f32[4,1024]{1,0:T(4,128)}, f32[4,1024]{1,0:T(4,128)S(1)}, u32[]{:S(2)}, u32[]{:S(2)}) collective-permute-start(f32[4,1024]{1,0:T(4,128)} %refs_1_.1), channel_id=1, source_target_pairs={{0,1},{1,0},{2,3},{3,2},{4,5},{5,4},{6,7},{7,6},{8,9},{9,8},{10,11... | collective-permute-start | bytes 49160 | tf_op jit(solution)/shard_map/ppermute | solution.py:177
  3.0 2.0 %prepare.1 = (f32[40,2048]{1,0:T(8,128)S(1)}, f32[4,1024]{1,0:T(4,128)S(1)}, s32[4,2048]{1,0:T(4,128)S(1)}, f32[4,2048]{1,0:T(4,128)S(1)}, f32[48,512]{1,0:T(8,1...) custom-call(f32[40,2048]{1,0:T(8,128)} %bitcast.4, f32[4,1024]{1,0:T(4,128)} %refs_1_.1, ...), custom_call_target="tpu_custom_call" | custom-call | flops 167772160 | bytes 655360 | tf_op jit(solution)/shard_map/prepare/pallas_call | solution.py:211
  5.0 0.0 collective-permute-done.refs_5_
  5.0 0.3 %send.1 = (f32[48,128]{1,0:T(8,128)S(1)}, f32[48,128]{1,0:T(8,128)S(1)}, f32[48,128]{1,0:T(8,128)S(1)}, f32[48,128]{1,0:T(8,128)S(1)}, f32[4,2048]{1,0:T(4,128)S(1)}) custom-call(f32[48,512]{1,0:T(8,128)S(1)} %get-tuple-element.19.refs_0_, bf16[128,512]{1,0:T(8,128)(2,1)S(1)} %get-tuple-element.20.refs_1_, bf16[128,512]{1,0:T(8,128)(2,1)S(1)} %get-tuple-element.21.refs_2_, ...), custom_call_target="tpu_custom_call" | custom-call | tf_op jit(solution)/shard_map/send/pallas_call | solution.py:237
  5.3 2.0 %collective-permute-start.1 = (f32[48,128]{1,0:T(8,128)S(1)}, f32[48,128]{1,0:T(8,128)S(1)}, u32[]{:S(2)}, u32[]{:S(2)}) collective-permute-start(f32[48,128]{1,0:T(8,128)S(1)} %get-tuple-element.25), channel_id=1, source_target_pairs={{0,2},{2,4},{4,6},{6,14},{8,0},{10,8},{12,10},{14,12},{16,18},{18,... | collective-permute-start | bytes 73736 | tf_op jit(solution)/shard_map/ppermute | solution.py:188
  7.3 0.0 collective-permute-start.2
  7.3 0.0 collective-permute-start.3
  7.3 1.6 %collective-permute-start.4 = (f32[48,128]{1,0:T(8,128)S(1)}, f32[48,128]{1,0:T(8,128)S(1)}, u32[]{:S(2)}, u32[]{:S(2)}) collective-permute-start(f32[48,128]{1,0:T(8,128)S(1)} %get-tuple-element.28), channel_id=1, source_target_pairs={{0,24},{8,16},{16,8},{24,0},{1,25},{9,17},{17,9},{25,1},{2,26},{10... | collective-permute-start | bytes 73736 | tf_op jit(solution)/shard_map/ppermute | solution.py:194
  8.9 2.9 %local.1.acc_ref = f32[640,256]{1,0:T(8,128)S(1)} custom-call(f32[40,2048]{1,0:T(8,128)S(1)} %get-tuple-element.17.u_ref, s32[4,2048]{1,0:T(4,128)S(1)} %get-tuple-element.18.dep_ref, f32[4,2048]{1,0:T(4,128)S(1)} %get-tuple-element.24.w_ref), custom_call_target="tpu_custom_call" | custom-call | flops 2684354560 | bytes 655360 | tf_op jit(solution)/shard_map/local/pallas_call | solution.py:260
  11.8 0.0 collective-permute-done.1.refs_0_
  11.9 0.0 collective-permute-done.2.refs_1_
  11.9 0.0 collective-permute-done.3.refs_2_
  11.9 0.0 collective-permute-done.4.refs_3_
  11.9 1.1 %arrive.1 = f32[40,2048]{1,0:T(8,128)} custom-call(f32[640,256]{1,0:T(8,128)S(1)} %local.1.acc_ref, f32[48,128]{1,0:T(8,128)S(1)} %collective-permute-done.1.refs_0_, f32[48,128]{1,0:T(8,128)S(1)} %collective-permute-done.2.refs_1_, f32[48,128]{1,0:T(8,128)S(1)} %collective-permute-done.3.refs_2_, f32[48,128]{1,0:T(8,128)S(1)} %collective-permute-done.4.refs_3_), custom_call_target="tpu_custom_call" | custom-call | tf_op jit(solution)/shard_map/arrive/pallas_call | solution.py:271
Async XLA Ops:
  0.0 5.0 %collective-permute-start = (f32[4,1024]{1,0:T(4,128)}, f32[4,1024]{1,0:T(4,128)S(1)}, u32[]{:S(2)}, u32[]{:S(2)}) collective-permute-start(f32[4,1024]{1,0:T(4,128)} %refs_1_.1), channel_id=1, source_target_pairs={{0,1},{1,0},{2,3},{3,2},{4,5},{5,4},{6,7},{7,6},{8,9},{9,8},{10,11... | collective-permute-start | bytes 49160 | tf_op jit(solution)/shard_map/ppermute | solution.py:177
  5.3 6.6 %collective-permute-start.1 = (f32[48,128]{1,0:T(8,128)S(1)}, f32[48,128]{1,0:T(8,128)S(1)}, u32[]{:S(2)}, u32[]{:S(2)}) collective-permute-start(f32[48,128]{1,0:T(8,128)S(1)} %get-tuple-element.25), channel_id=1, source_target_pairs={{0,2},{2,4},{4,6},{6,14},{8,0},{10,8},{12,10},{14,12},{16,18},{18,... | collective-permute-start | bytes 73736 | tf_op jit(solution)/shard_map/ppermute | solution.py:188
  7.3 4.6 %collective-permute-start.2 = (f32[48,128]{1,0:T(8,128)S(1)}, f32[48,128]{1,0:T(8,128)S(1)}, u32[]{:S(2)}, u32[]{:S(2)}) collective-permute-start(f32[48,128]{1,0:T(8,128)S(1)} %get-tuple-element.26), channel_id=1, source_target_pairs={{0,8},{2,0},{4,2},{6,4},{8,10},{10,12},{12,14},{14,6},{16,24},{18,... | collective-permute-start | bytes 73736 | tf_op jit(solution)/shard_map/ppermute | solution.py:188
  7.3 4.6 %collective-permute-start.3 = (f32[48,128]{1,0:T(8,128)S(1)}, f32[48,128]{1,0:T(8,128)S(1)}, u32[]{:S(2)}, u32[]{:S(2)}) collective-permute-start(f32[48,128]{1,0:T(8,128)S(1)} %get-tuple-element.27), channel_id=1, source_target_pairs={{0,8},{8,0},{16,24},{24,16},{1,9},{9,1},{17,25},{25,17},{2,10},{10... | collective-permute-start | bytes 73736 | tf_op jit(solution)/shard_map/ppermute | solution.py:194
  7.3 4.6 %collective-permute-start.4 = (f32[48,128]{1,0:T(8,128)S(1)}, f32[48,128]{1,0:T(8,128)S(1)}, u32[]{:S(2)}, u32[]{:S(2)}) collective-permute-start(f32[48,128]{1,0:T(8,128)S(1)} %get-tuple-element.28), channel_id=1, source_target_pairs={{0,24},{8,16},{16,8},{24,0},{1,25},{9,17},{17,9},{25,1},{2,26},{10... | collective-permute-start | bytes 73736 | tf_op jit(solution)/shard_map/ppermute | solution.py:194

commit v4 on v3

--- a/solution.py
+++ b/solution.py
@@ -37,9 +37,19 @@
     return lax.dot_general(left, jnp.concatenate(right, axis=1), NT, preferred_element_type=F32)
 
 
+def piece(steps, width):
+    count = lax.axis_size("lev")
+    source = lax.rem(lax.axis_index("lev") + (count - steps), count)
+    return pl.ds(pl.multiple_of(source * width, LANES), width)
+
+
+def scattered(u_ref, dep_ref, weight, k, at):
+    return two_terms(u_ref[:, at] * weight).astype(BF16), dep_ref[k : k + 1, at]
+
+
 def prepare_kernel(
-    levels, u_hbm, w_hbm, dep_hbm, sp_hbm, bc_hbm, rot_hbm,
-    u_ref, w_ref, dep_ref, keep_ref, picked_ref, live_ref, lane_ref,
+    levels, early, u_hbm, w_hbm, dep_hbm, sp_hbm, bc_hbm, rot_hbm,
+    u_ref, w_ref, dep_ref, keep_ref, picked_ref, live_ref, lane_ref, acc_ref,
     sp_ref, bc_ref, rot_ref, sems,
 ):
     pairs = [(sp_hbm, sp_ref), (bc_hbm, bc_ref), (rot_hbm, rot_ref), (dep_hbm, dep_ref), (u_hbm, u_ref), (w_hbm, w_ref)]
@@ -70,7 +80,6 @@
     sent = lax.dot_general(live, lane, NT, preferred_element_type=F32)
     for t in range(tiles):
         keep_ref[:, t * LANES : (t + 1) * LANES] = 1.0 - sent[t * SUB : t * SUB + stencil]
-    onehot = one_hot(cells, jnp.concatenate(columns, axis=1))
     for c in copies[3:]:
         c.wait()
     dep = dep_ref[...]
@@ -80,6 +89,7 @@
         [two_terms(u_ref[...]), jnp.concatenate([dep_high.astype(F32), dep_low.astype(F32)], axis=0), jnp.zeros((SUB, cells), F32)],
         axis=0,
     ).astype(BF16)
+    onehot = one_hot(cells, jnp.concatenate(columns, axis=1))
     got = jnp.dot(table, onehot, preferred_element_type=F32)
     at = 2 * rows
     for j in range(blocks):
@@ -100,15 +110,10 @@
         picked_ref[levels : 2 * levels, here] = merid
         picked_ref[2 * levels : rows, here] = values[2 * levels :]
         picked_ref[rows:, here] = jnp.broadcast_to(ids, (SUB, slots))
-
-
-def place_weights(parts, full):
-    count = len(parts)
-    width = parts[0].shape[1]
-    me = lax.axis_index("lev")
-    for s, part in enumerate(parts):
-        source = lax.rem(me + (count - s), count)
-        full[:, pl.ds(pl.multiple_of(source * width, LANES), width)] = part[...]
+    own = piece(0, w_ref.shape[1])
+    acc_ref[...] = scatter_product(
+        [scattered(u_ref, dep_ref, w_ref[k : k + 1, :] * keep_ref[k : k + 1, own], k, own) for k in range(early)], cells
+    )
 
 
 def send_kernel(count, paired, picked_ref, live_ref, lane_ref, keep_ref, *refs):
@@ -116,7 +121,8 @@
     stencil, cells = full.shape
     rows = picked_ref.shape[0] - SUB
     blocks, slots = len(outs), outs[0].shape[1]
-    place_weights(parts, full)
+    for steps, part in enumerate(parts):
+        full[:, piece(steps, part.shape[1])] = part[...]
     pad = jnp.zeros((SUB - stencil, LANES), F32)
     pieces = []
     for t in range(cells // LANES):
@@ -150,14 +156,12 @@
     masked_ref[...] = full[...] * keep_ref[...]
 
 
-def local_kernel(u_ref, dep_ref, w_ref, acc_ref):
-    cells = u_ref.shape[1]
-    acc_ref[...] = scatter_product(
-        [
-            (two_terms(u_ref[...] * w_ref[k : k + 1, :]).astype(BF16), dep_ref[k : k + 1, :])
-            for k in range(dep_ref.shape[0])
-        ],
-        cells,
+def local_kernel(early, count, u_ref, dep_ref, w_ref, early_ref, acc_ref):
+    stencil, cells = dep_ref.shape
+    at = [(k, piece(s, cells // count)) for k in range(early) for s in range(1, count)]
+    at += [(k, slice(None)) for k in range(early, stencil)]
+    acc_ref[...] = early_ref[...] + scatter_product(
+        [scattered(u_ref, dep_ref, w_ref[k : k + 1, here], k, here) for k, here in at], cells
     )
 
 
@@ -202,14 +206,16 @@
     count = lax.axis_size("lev")
     paired = lax.axis_size("panel") % 2 == 0
     points = blocks * slots
+    early = stencil // 2
     shape = jax.ShapeDtypeStruct
     parts = [rotated(weights, "lev", s) for s in range(1, count)]
     inputs = (
         adjoint_new.reshape(rows, cells), weights, departure, send_point,
         block_count.reshape(1, -1), rotation.reshape(1, -1),
     )
-    u, own, dep, keep, picked, live, lane = pl.pallas_call(
-        lambda *refs: prepare_kernel(levels, *refs),
+    sums = shape((cells // LO * 2 * rows, LO), F32)
+    u, own, dep, keep, picked, live, lane, acc = pl.pallas_call(
+        lambda *refs: prepare_kernel(levels, early, *refs),
         out_shape=[
             shape((rows, cells), F32),
             shape(weights.shape, F32),
@@ -218,9 +224,10 @@
             shape((rows + SUB, points), F32),
             shape((cells // LANES * SUB, points), BF16),
             shape((LANES, points), BF16),
+            sums,
         ],
         in_specs=[HBM] * 6,
-        out_specs=[VMEM] * 7,
+        out_specs=[VMEM] * 8,
         scratch_shapes=[
             pltpu.VMEM((blocks, slots), I32),
             pltpu.VMEM((1, block_count.size), I32),
@@ -258,16 +265,16 @@
             rotated(outgoing[2], "panel", -1),
         ]
     local = pl.pallas_call(
-        local_kernel,
-        out_shape=shape((cells // LO * 2 * rows, LO), F32),
-        in_specs=[VMEM] * 3,
+        lambda *refs: local_kernel(early, count, *refs),
+        out_shape=sums,
+        in_specs=[VMEM] * 4,
         out_specs=VMEM,
         cost_estimate=pl.CostEstimate(
             flops=4 * rows * cells * stencil * cells, bytes_accessed=8 * rows * cells, transcendentals=0
         ),
         compiler_params=PARAMS,
         name="local",
-    )(u, dep, masked)
+    )(u, dep, masked, acc)
     out = pl.pallas_call(
         arrive_kernel,
         out_shape=shape((rows, cells), F32),

time: 13.2 us -> 12.5 us (0.947)
  starting transfers between devices: 6.64 us -> 6.26 us
  Pallas kernels: 6.32 us -> 6.02 us
    ppermute x2, starting transfers between devices: 2.04 us -> 1.66 us  [racetrack(): return lax.ppermute(value, ('panel', 'tile'), route)]
    pallas_call x2, Pallas kernels: 4.91 us -> 4.61 us  [the longest x1 2.37 us: body(): pl.pallas_call(lambda *refs: prepare_kernel(levels, early, *refs), out_sh...]
  transfers between devices with their start and end apart: 5 -> 5, of which waited for: 0 -> 0; matrix products, arithmetic and copies ran while one was open for 0% -> 0% of each run, Pallas kernels for 38% -> 37%
where the time goes in v4:
time: 12.5 us; the launch traced here: 12.4 us
  starting transfers between devices  6.26 us (50%)
  Pallas kernels  6.02 us (48%)
    ppermute x1, starting transfers between devices, rotated(): lax.ppermute(value, axis, [(i, (i + steps) % count) for i in range(count)])  2.97 us
    pallas_call x1, Pallas kernels, body(): pl.pallas_call(lambda *refs: prepare_kernel(levels, early, *refs), out_sh...  2.37 us
    pallas_call x1, Pallas kernels, body(): pl.pallas_call(lambda *refs: local_kernel(early, count, *refs), out_shape...  2.24 us
    ppermute x2, starting transfers between devices, racetrack(): return lax.ppermute(value, ('panel', 'tile'), route)  1.66 us
    ppermute x2, starting transfers between devices, swapped(): lax.ppermute(value, 'panel', [(i, (i + step[i % 2]) % count) for i in ran...  1.63 us
    pallas_call x1, Pallas kernels, body(): pl.pallas_call(arrive_kernel, out_shape=shape((rows, cells), F32), in_spe...  1.14 us
    pallas_call x1, Pallas kernels, body(): pl.pallas_call(lambda *refs: send_kernel(count, paired, *refs), out_shape...  0.27 us
  transfers between devices with their start and end apart: 5, of which 0 were waited for; matrix products, arithmetic and copies ran while one was open for 0% of the time, Pallas kernels for 37%

profile of v4, /device:TPU:0, one launch (start us, length us, event | category | flops | bytes accessed | tf_op | source)
XLA Modules:
  0.0 12.4 jit_solution(11720295906217082532)
XLA Ops:
  0.0 3.0 %collective-permute-start = (f32[4,1024]{1,0:T(4,128)}, f32[4,1024]{1,0:T(4,128)S(1)}, u32[]{:S(2)}, u32[]{:S(2)}) collective-permute-start(f32[4,1024]{1,0:T(4,128)} %refs_1_.1), channel_id=1, source_target_pairs={{0,1},{1,0},{2,3},{3,2},{4,5},{5,4},{6,7},{7,6},{8,9},{9,8},{10,11... | collective-permute-start | bytes 49160 | tf_op jit(solution)/shard_map/ppermute | solution.py:181
  3.0 2.4 %prepare.1 = (f32[40,2048]{1,0:T(8,128)S(1)}, f32[4,1024]{1,0:T(4,128)S(1)}, s32[4,2048]{1,0:T(4,128)S(1)}, f32[4,2048]{1,0:T(4,128)S(1)}, f32[48,512]{1,0:T(8,1...) custom-call(f32[40,2048]{1,0:T(8,128)} %bitcast.4, ...), custom_call_target="tpu_custom_call" | custom-call | flops 167772160 | bytes 655360 | tf_op jit(solution)/shard_map/prepare/pallas_call | solution.py:217
  5.3 0.0 collective-permute-done.refs_5_
  5.4 0.3 %send.1 = (f32[48,128]{1,0:T(8,128)S(1)}, f32[48,128]{1,0:T(8,128)S(1)}, f32[48,128]{1,0:T(8,128)S(1)}, f32[48,128]{1,0:T(8,128)S(1)}, f32[4,2048]{1,0:T(4,128)S(1)}) custom-call(f32[48,512]{1,0:T(8,128)S(1)} %get-tuple-element.20.refs_0_, bf16[128,512]{1,0:T(8,128)(2,1)S(1)} %get-tuple-element.21.refs_1_, bf16[128,512]{1,0:T(8,128)(2,1)S(1)} %get-tuple-element.22.refs_2_, ...), custom_call_target="tpu_custom_call" | custom-call | tf_op jit(solution)/shard_map/send/pallas_call | solution.py:244
  5.6 1.7 %collective-permute-start.1 = (f32[48,128]{1,0:T(8,128)S(1)}, f32[48,128]{1,0:T(8,128)S(1)}, u32[]{:S(2)}, u32[]{:S(2)}) collective-permute-start(f32[48,128]{1,0:T(8,128)S(1)} %get-tuple-element.27), channel_id=1, source_target_pairs={{0,2},{2,4},{4,6},{6,14},{8,0},{10,8},{12,10},{14,12},{16,18},{18,... | collective-permute-start | bytes 73736 | tf_op jit(solution)/shard_map/ppermute | solution.py:192
  7.3 0.0 collective-permute-start.2
  7.3 0.0 collective-permute-start.3
  7.3 1.6 %collective-permute-start.4 = (f32[48,128]{1,0:T(8,128)S(1)}, f32[48,128]{1,0:T(8,128)S(1)}, u32[]{:S(2)}, u32[]{:S(2)}) collective-permute-start(f32[48,128]{1,0:T(8,128)S(1)} %get-tuple-element.30), channel_id=1, source_target_pairs={{0,24},{8,16},{16,8},{24,0},{1,25},{9,17},{17,9},{25,1},{2,26},{10... | collective-permute-start | bytes 73736 | tf_op jit(solution)/shard_map/ppermute | solution.py:198
  8.9 2.2 %local.1.acc_ref = f32[640,256]{1,0:T(8,128)S(1)} custom-call(f32[40,2048]{1,0:T(8,128)S(1)} %get-tuple-element.18.refs_0_, s32[4,2048]{1,0:T(4,128)S(1)} %get-tuple-element.19.refs_1_, f32[4,2048]{1,0:T(4,128)S(1)} %get-tuple-element.25.refs_2_, f32[640,256]{1,0:T(8,128)S(1)} %get-tuple-element.26.refs_3_), custom_call_target="tpu_custom_call" | custom-call | flops 2684354560 | bytes 655360 | tf_op jit(solution)/shard_map/local/pallas_call | solution.py:267
  11.2 0.0 collective-permute-done.1.refs_0_
  11.2 0.0 collective-permute-done.2.refs_1_
  11.2 0.0 collective-permute-done.3.refs_2_
  11.2 0.0 collective-permute-done.4.refs_3_
  11.2 1.1 %arrive.1 = f32[40,2048]{1,0:T(8,128)} custom-call(f32[640,256]{1,0:T(8,128)S(1)} %local.1.acc_ref, f32[48,128]{1,0:T(8,128)S(1)} %collective-permute-done.1.refs_0_, f32[48,128]{1,0:T(8,128)S(1)} %collective-permute-done.2.refs_1_, f32[48,128]{1,0:T(8,128)S(1)} %collective-permute-done.3.refs_2_, f32[48,128]{1,0:T(8,128)S(1)} %collective-permute-done.4.refs_3_), custom_call_target="tpu_custom_call" | custom-call | tf_op jit(solution)/shard_map/arrive/pallas_call | solution.py:278
Async XLA Ops:
  0.0 5.3 %collective-permute-start = (f32[4,1024]{1,0:T(4,128)}, f32[4,1024]{1,0:T(4,128)S(1)}, u32[]{:S(2)}, u32[]{:S(2)}) collective-permute-start(f32[4,1024]{1,0:T(4,128)} %refs_1_.1), channel_id=1, source_target_pairs={{0,1},{1,0},{2,3},{3,2},{4,5},{5,4},{6,7},{7,6},{8,9},{9,8},{10,11... | collective-permute-start | bytes 49160 | tf_op jit(solution)/shard_map/ppermute | solution.py:181
  5.6 5.5 %collective-permute-start.1 = (f32[48,128]{1,0:T(8,128)S(1)}, f32[48,128]{1,0:T(8,128)S(1)}, u32[]{:S(2)}, u32[]{:S(2)}) collective-permute-start(f32[48,128]{1,0:T(8,128)S(1)} %get-tuple-element.27), channel_id=1, source_target_pairs={{0,2},{2,4},{4,6},{6,14},{8,0},{10,8},{12,10},{14,12},{16,18},{18,... | collective-permute-start | bytes 73736 | tf_op jit(solution)/shard_map/ppermute | solution.py:192
  7.3 3.9 %collective-permute-start.2 = (f32[48,128]{1,0:T(8,128)S(1)}, f32[48,128]{1,0:T(8,128)S(1)}, u32[]{:S(2)}, u32[]{:S(2)}) collective-permute-start(f32[48,128]{1,0:T(8,128)S(1)} %get-tuple-element.28), channel_id=1, source_target_pairs={{0,8},{2,0},{4,2},{6,4},{8,10},{10,12},{12,14},{14,6},{16,24},{18,... | collective-permute-start | bytes 73736 | tf_op jit(solution)/shard_map/ppermute | solution.py:192
  7.3 3.9 %collective-permute-start.3 = (f32[48,128]{1,0:T(8,128)S(1)}, f32[48,128]{1,0:T(8,128)S(1)}, u32[]{:S(2)}, u32[]{:S(2)}) collective-permute-start(f32[48,128]{1,0:T(8,128)S(1)} %get-tuple-element.29), channel_id=1, source_target_pairs={{0,8},{8,0},{16,24},{24,16},{1,9},{9,1},{17,25},{25,17},{2,10},{10... | collective-permute-start | bytes 73736 | tf_op jit(solution)/shard_map/ppermute | solution.py:198
  7.3 3.9 %collective-permute-start.4 = (f32[48,128]{1,0:T(8,128)S(1)}, f32[48,128]{1,0:T(8,128)S(1)}, u32[]{:S(2)}, u32[]{:S(2)}) collective-permute-start(f32[48,128]{1,0:T(8,128)S(1)} %get-tuple-element.30), channel_id=1, source_target_pairs={{0,24},{8,16},{16,8},{24,0},{1,25},{9,17},{17,9},{25,1},{2,26},{10... | collective-permute-start | bytes 73736 | tf_op jit(solution)/shard_map/ppermute | solution.py:198

commit v5 on v4

--- a/solution.py
+++ b/solution.py
@@ -86,21 +86,33 @@
     dep_high = dep // SUB
     dep_low = dep - dep_high * SUB
     table = jnp.concatenate(
-        [two_terms(u_ref[...]), jnp.concatenate([dep_high.astype(F32), dep_low.astype(F32)], axis=0), jnp.zeros((SUB, cells), F32)],
+        [two_terms(u_ref[...]), dep_high.astype(F32), dep_low.astype(F32), jnp.zeros((SUB, cells), F32)],
         axis=0,
     ).astype(BF16)
-    onehot = one_hot(cells, jnp.concatenate(columns, axis=1))
-    got = jnp.dot(table, onehot, preferred_element_type=F32)
-    at = 2 * rows
+    column = jnp.concatenate(columns, axis=1)
+    chunk = column // LO
+    height = table.shape[0]
+    got = jnp.dot(
+        jnp.concatenate([table[:, c * LO : (c + 1) * LO] for c in range(cells // LO)], axis=0),
+        one_hot(LO, column - chunk * LO),
+        preferred_element_type=F32,
+    )
+    values = jnp.zeros((rows, blocks * slots), F32)
+    targets = jnp.zeros((2 * stencil, blocks * slots), F32)
+    for c in range(cells // LO):
+        at = c * height
+        here = chunk == c
+        values = values + jnp.where(here, got[at : at + rows] + got[at + rows : at + 2 * rows], 0.0)
+        targets = targets + jnp.where(here, got[at + 2 * rows : at + 2 * rows + 2 * stencil], 0.0)
+    k = jnp.concatenate(which, axis=1)
+    ids = jnp.zeros((1, blocks * slots), F32)
+    for i in range(stencil):
+        ids = ids + jnp.where(k == i, targets[i : i + 1] * SUB + targets[stencil + i : stencil + i + 1], 0.0)
+    picked_ref[rows:, :] = jnp.broadcast_to(ids, (SUB, blocks * slots))
+    picked_ref[2 * levels : rows, :] = values[2 * levels :]
     for j in range(blocks):
         here = slice(j * slots, (j + 1) * slots)
-        g = got[:, here]
-        ids = jnp.zeros((1, slots), F32)
-        for k in range(stencil):
-            one_id = g[at + k : at + k + 1] * SUB + g[at + stencil + k : at + stencil + k + 1]
-            ids = ids + jnp.where(which[j] == k, one_id, 0.0)
-        values = g[:rows] + g[rows : 2 * rows]
-        zonal, merid = values[:levels], values[levels : 2 * levels]
+        zonal, merid = values[:levels, here], values[levels : 2 * levels, here]
         if j >= 2:
             code = rot_ref[0:1, j - 2 : j - 1]
             cosine = (code == 0).astype(F32) - (code == 2).astype(F32)
@@ -108,8 +120,6 @@
             zonal, merid = cosine * zonal + sine * merid, cosine * merid - sine * zonal
         picked_ref[:levels, here] = zonal
         picked_ref[levels : 2 * levels, here] = merid
-        picked_ref[2 * levels : rows, here] = values[2 * levels :]
-        picked_ref[rows:, here] = jnp.broadcast_to(ids, (SUB, slots))
     own = piece(0, w_ref.shape[1])
     acc_ref[...] = scatter_product(
         [scattered(u_ref, dep_ref, w_ref[k : k + 1, :] * keep_ref[k : k + 1, own], k, own) for k in range(early)], cells
@@ -252,10 +262,10 @@
     )(picked, live, lane, keep, own, *parts)
     if paired:
         received = [
+            swapped(outgoing[3], True),
+            racetrack(outgoing[1], True),
             racetrack(outgoing[0], False),
-            racetrack(outgoing[1], True),
             swapped(outgoing[2], False),
-            swapped(outgoing[3], True),
         ]
     else:
         received = [

time: 12.5 us -> 12.3 us (0.984)
  Pallas kernels: 6.02 us -> 5.86 us
    ppermute x2, starting transfers between devices: 1.63 us -> 1.2 us  [swapped(): lax.ppermute(value, 'panel', [(i, (i + step[i % 2]) % count) for i in ran...]
    ppermute x2, starting transfers between devices: 1.66 us -> 2.03 us  [racetrack(): return lax.ppermute(value, ('panel', 'tile'), route)]
    pallas_call x1, Pallas kernels: 2.37 us -> 2.21 us  [body(): pl.pallas_call(lambda *refs: prepare_kernel(levels, early, *refs), out_sh...]
where the time goes in v5:
time: 12.3 us; the launch traced here: 12.1 us
  starting transfers between devices  6.19 us (50%)
  Pallas kernels  5.86 us (48%)
    ppermute x1, starting transfers between devices, rotated(): lax.ppermute(value, axis, [(i, (i + steps) % count) for i in range(count)])  2.97 us
    pallas_call x1, Pallas kernels, body(): pl.pallas_call(lambda *refs: local_kernel(early, count, *refs), out_shape...  2.24 us
    pallas_call x1, Pallas kernels, body(): pl.pallas_call(lambda *refs: prepare_kernel(levels, early, *refs), out_sh...  2.21 us
    ppermute x2, starting transfers between devices, racetrack(): return lax.ppermute(value, ('panel', 'tile'), route)  2.03 us
    ppermute x2, starting transfers between devices, swapped(): lax.ppermute(value, 'panel', [(i, (i + step[i % 2]) % count) for i in ran...  1.2 us
    pallas_call x1, Pallas kernels, body(): pl.pallas_call(arrive_kernel, out_shape=shape((rows, cells), F32), in_spe...  1.14 us
    pallas_call x1, Pallas kernels, body(): pl.pallas_call(lambda *refs: send_kernel(count, paired, *refs), out_shape...  0.27 us
  transfers between devices with their start and end apart: 5, of which 0 were waited for; matrix products, arithmetic and copies ran while one was open for 0% of the time, Pallas kernels for 37%

profile of v5, /device:TPU:0, one launch (start us, length us, event | category | flops | bytes accessed | tf_op | source)
XLA Modules:
  0.0 12.1 jit_solution(9829129428491666503)
XLA Ops:
  0.0 3.0 %collective-permute-start = (f32[4,1024]{1,0:T(4,128)}, f32[4,1024]{1,0:T(4,128)S(1)}, u32[]{:S(2)}, u32[]{:S(2)}) collective-permute-start(f32[4,1024]{1,0:T(4,128)} %refs_1_.1), channel_id=1, source_target_pairs={{0,1},{1,0},{2,3},{3,2},{4,5},{5,4},{6,7},{7,6},{8,9},{9,8},{10,11... | collective-permute-start | bytes 49160 | tf_op jit(solution)/shard_map/ppermute | solution.py:191
  3.0 2.2 %prepare.1 = (f32[40,2048]{1,0:T(8,128)S(1)}, f32[4,1024]{1,0:T(4,128)S(1)}, s32[4,2048]{1,0:T(4,128)S(1)}, f32[4,2048]{1,0:T(4,128)S(1)}, f32[48,512]{1,0:T(8,1...) custom-call(f32[40,2048]{1,0:T(8,128)} %bitcast.4, ...), custom_call_target="tpu_custom_call" | custom-call | flops 167772160 | bytes 655360 | tf_op jit(solution)/shard_map/prepare/pallas_call | solution.py:227
  5.2 0.0 collective-permute-done.refs_5_
  5.2 0.3 %send.1 = (f32[48,128]{1,0:T(8,128)S(1)}, f32[48,128]{1,0:T(8,128)S(1)}, f32[48,128]{1,0:T(8,128)S(1)}, f32[48,128]{1,0:T(8,128)S(1)}, f32[4,2048]{1,0:T(4,128)S(1)}) custom-call(f32[48,512]{1,0:T(8,128)S(1)} %get-tuple-element.20.refs_0_, bf16[128,512]{1,0:T(8,128)(2,1)S(1)} %get-tuple-element.21.refs_1_, bf16[128,512]{1,0:T(8,128)(2,1)S(1)} %get-tuple-element.22.refs_2_, ...), custom_call_target="tpu_custom_call" | custom-call | tf_op jit(solution)/shard_map/send/pallas_call | solution.py:254
  5.5 0.7 %collective-permute-start.1 = (f32[48,128]{1,0:T(8,128)S(1)}, f32[48,128]{1,0:T(8,128)S(1)}, u32[]{:S(2)}, u32[]{:S(2)}) collective-permute-start(f32[48,128]{1,0:T(8,128)S(1)} %get-tuple-element.27), channel_id=1, source_target_pairs={{0,24},{8,16},{16,8},{24,0},{1,25},{9,17},{17,9},{25,1},{2,26},{10... | collective-permute-start | bytes 73736 | tf_op jit(solution)/shard_map/ppermute | solution.py:208
  6.2 1.2 %collective-permute-start.2 = (f32[48,128]{1,0:T(8,128)S(1)}, f32[48,128]{1,0:T(8,128)S(1)}, u32[]{:S(2)}, u32[]{:S(2)}) collective-permute-start(f32[48,128]{1,0:T(8,128)S(1)} %get-tuple-element.28), channel_id=1, source_target_pairs={{0,8},{2,0},{4,2},{6,4},{8,10},{10,12},{12,14},{14,6},{16,24},{18,... | collective-permute-start | bytes 73736 | tf_op jit(solution)/shard_map/ppermute | solution.py:202
  7.4 0.8 %collective-permute-start.3 = (f32[48,128]{1,0:T(8,128)S(1)}, f32[48,128]{1,0:T(8,128)S(1)}, u32[]{:S(2)}, u32[]{:S(2)}) collective-permute-start(f32[48,128]{1,0:T(8,128)S(1)} %get-tuple-element.29), channel_id=1, source_target_pairs={{0,2},{2,4},{4,6},{6,14},{8,0},{10,8},{12,10},{14,12},{16,18},{18,... | collective-permute-start | bytes 73736 | tf_op jit(solution)/shard_map/ppermute | solution.py:202
  8.2 0.5 %collective-permute-start.4 = (f32[48,128]{1,0:T(8,128)S(1)}, f32[48,128]{1,0:T(8,128)S(1)}, u32[]{:S(2)}, u32[]{:S(2)}) collective-permute-start(f32[48,128]{1,0:T(8,128)S(1)} %get-tuple-element.30), channel_id=1, source_target_pairs={{0,8},{8,0},{16,24},{24,16},{1,9},{9,1},{17,25},{25,17},{2,10},{10... | collective-permute-start | bytes 73736 | tf_op jit(solution)/shard_map/ppermute | solution.py:208
  8.7 2.2 %local.1.acc_ref = f32[640,256]{1,0:T(8,128)S(1)} custom-call(f32[40,2048]{1,0:T(8,128)S(1)} %get-tuple-element.18.refs_0_, s32[4,2048]{1,0:T(4,128)S(1)} %get-tuple-element.19.refs_1_, f32[4,2048]{1,0:T(4,128)S(1)} %get-tuple-element.25.refs_2_, f32[640,256]{1,0:T(8,128)S(1)} %get-tuple-element.26.refs_3_), custom_call_target="tpu_custom_call" | custom-call | flops 2684354560 | bytes 655360 | tf_op jit(solution)/shard_map/local/pallas_call | solution.py:277
  11.0 0.0 collective-permute-done.1.refs_0_
  11.0 0.0 collective-permute-done.2.refs_1_
  11.0 0.0 collective-permute-done.3.refs_2_
  11.0 0.0 collective-permute-done.4.refs_3_
  11.0 1.1 %arrive.1 = f32[40,2048]{1,0:T(8,128)} custom-call(f32[640,256]{1,0:T(8,128)S(1)} %local.1.acc_ref, f32[48,128]{1,0:T(8,128)S(1)} %collective-permute-done.1.refs_0_, f32[48,128]{1,0:T(8,128)S(1)} %collective-permute-done.2.refs_1_, f32[48,128]{1,0:T(8,128)S(1)} %collective-permute-done.3.refs_2_, f32[48,128]{1,0:T(8,128)S(1)} %collective-permute-done.4.refs_3_), custom_call_target="tpu_custom_call" | custom-call | tf_op jit(solution)/shard_map/arrive/pallas_call | solution.py:288
Async XLA Ops:
  0.0 5.2 %collective-permute-start = (f32[4,1024]{1,0:T(4,128)}, f32[4,1024]{1,0:T(4,128)S(1)}, u32[]{:S(2)}, u32[]{:S(2)}) collective-permute-start(f32[4,1024]{1,0:T(4,128)} %refs_1_.1), channel_id=1, source_target_pairs={{0,1},{1,0},{2,3},{3,2},{4,5},{5,4},{6,7},{7,6},{8,9},{9,8},{10,11... | collective-permute-start | bytes 49160 | tf_op jit(solution)/shard_map/ppermute | solution.py:191
  5.5 5.5 %collective-permute-start.1 = (f32[48,128]{1,0:T(8,128)S(1)}, f32[48,128]{1,0:T(8,128)S(1)}, u32[]{:S(2)}, u32[]{:S(2)}) collective-permute-start(f32[48,128]{1,0:T(8,128)S(1)} %get-tuple-element.27), channel_id=1, source_target_pairs={{0,24},{8,16},{16,8},{24,0},{1,25},{9,17},{17,9},{25,1},{2,26},{10... | collective-permute-start | bytes 73736 | tf_op jit(solution)/shard_map/ppermute | solution.py:208
  6.2 4.7 %collective-permute-start.2 = (f32[48,128]{1,0:T(8,128)S(1)}, f32[48,128]{1,0:T(8,128)S(1)}, u32[]{:S(2)}, u32[]{:S(2)}) collective-permute-start(f32[48,128]{1,0:T(8,128)S(1)} %get-tuple-element.28), channel_id=1, source_target_pairs={{0,8},{2,0},{4,2},{6,4},{8,10},{10,12},{12,14},{14,6},{16,24},{18,... | collective-permute-start | bytes 73736 | tf_op jit(solution)/shard_map/ppermute | solution.py:202
  7.4 3.6 %collective-permute-start.3 = (f32[48,128]{1,0:T(8,128)S(1)}, f32[48,128]{1,0:T(8,128)S(1)}, u32[]{:S(2)}, u32[]{:S(2)}) collective-permute-start(f32[48,128]{1,0:T(8,128)S(1)} %get-tuple-element.29), channel_id=1, source_target_pairs={{0,2},{2,4},{4,6},{6,14},{8,0},{10,8},{12,10},{14,12},{16,18},{18,... | collective-permute-start | bytes 73736 | tf_op jit(solution)/shard_map/ppermute | solution.py:202
  8.2 2.7 %collective-permute-start.4 = (f32[48,128]{1,0:T(8,128)S(1)}, f32[48,128]{1,0:T(8,128)S(1)}, u32[]{:S(2)}, u32[]{:S(2)}) collective-permute-start(f32[48,128]{1,0:T(8,128)S(1)} %get-tuple-element.30), channel_id=1, source_target_pairs={{0,8},{8,0},{16,24},{24,16},{1,9},{9,1},{17,25},{25,17},{2,10},{10... | collective-permute-start | bytes 73736 | tf_op jit(solution)/shard_map/ppermute | solution.py:208

commit v6 on v5

--- a/solution.py
+++ b/solution.py
@@ -152,15 +152,11 @@
         )
         for j in range(blocks)
     ]
+    low, high, previous, following = message
     if paired:
         even = lax.rem(lax.axis_index("panel"), 2) == 0
-        low, high, previous, following = message
-        message = [
-            jnp.where(even, high, low),
-            jnp.where(even, low, high),
-            jnp.where(even, following, previous),
-            jnp.where(even, previous, following),
-        ]
+        low, high = jnp.where(even, low, high), jnp.where(even, high, low)
+    message = [low, following, high, previous]
     for out, m in zip(outs, message):
         out[...] = m
     masked_ref[...] = full[...] * keep_ref[...]
@@ -202,12 +198,6 @@
     return lax.ppermute(value, ("panel", "tile"), route)
 
 
-def swapped(value, outer):
-    count = lax.axis_size("panel")
-    step = [1, -1] if not outer else [-1, 1]
-    return lax.ppermute(value, "panel", [(i, (i + step[i % 2]) % count) for i in range(count)])
-
-
 def body(adjoint_new, weights, departure, send_point, block_count, rotation):
     fields, levels, cells = adjoint_new.shape
     blocks, slots = send_point.shape
@@ -216,7 +206,7 @@
     count = lax.axis_size("lev")
     paired = lax.axis_size("panel") % 2 == 0
     points = blocks * slots
-    early = stencil // 2
+    early = 1
     shape = jax.ShapeDtypeStruct
     parts = [rotated(weights, "lev", s) for s in range(1, count)]
     inputs = (
@@ -261,19 +251,15 @@
         name="send",
     )(picked, live, lane, keep, own, *parts)
     if paired:
-        received = [
-            swapped(outgoing[3], True),
-            racetrack(outgoing[1], True),
-            racetrack(outgoing[0], False),
-            swapped(outgoing[2], False),
-        ]
+        back, forth = (lambda v: racetrack(v, True)), (lambda v: racetrack(v, False))
     else:
-        received = [
-            rotated(outgoing[1], "tile", 1),
-            rotated(outgoing[0], "tile", -1),
-            rotated(outgoing[3], "panel", 1),
-            rotated(outgoing[2], "panel", -1),
-        ]
+        back, forth = (lambda v: rotated(v, "tile", -1)), (lambda v: rotated(v, "tile", 1))
+    received = [
+        back(outgoing[0]),
+        rotated(outgoing[1], "panel", 1),
+        forth(outgoing[2]),
+        rotated(outgoing[3], "panel", -1),
+    ]
     local = pl.pallas_call(
         lambda *refs: local_kernel(early, count, *refs),
         out_shape=sums,

time: 12.3 us -> 11.7 us (0.951)
  the two profiles are of different devices: /device:TPU:0 before, /device:TPU:1 now
where the time goes in v6:
time: 11.7 us; the launch traced here: 11.5 us
  Pallas kernels  5.84 us (50%)
  starting transfers between devices  5.43 us (46%)
  waiting for transfers between devices  0.2 us (2%)
    ppermute x3, starting transfers between devices, rotated(): lax.ppermute(value, axis, [(i, (i + steps) % count) for i in range(count)])  4.11 us
    pallas_call x1, Pallas kernels, body(): pl.pallas_call(lambda *refs: local_kernel(early, count, *refs), out_shape...  2.58 us
    pallas_call x1, Pallas kernels, body(): pl.pallas_call(lambda *refs: prepare_kernel(levels, early, *refs), out_sh...  1.87 us
    ppermute x2, starting transfers between devices, racetrack(): return lax.ppermute(value, ('panel', 'tile'), route)  1.32 us
    pallas_call x1, Pallas kernels, body(): pl.pallas_call(arrive_kernel, out_shape=shape((rows, cells), F32), in_spe...  1.14 us
    pallas_call x1, Pallas kernels, body(): pl.pallas_call(lambda *refs: send_kernel(count, paired, *refs), out_shape...  0.26 us
  transfers between devices with their start and end apart: 5, of which 1 were waited for; matrix products, arithmetic and copies ran while one was open for 0% of the time, Pallas kernels for 39%

profile of v6, /device:TPU:1, one launch (start us, length us, event | category | flops | bytes accessed | tf_op | source)
XLA Modules:
  0.0 11.5 jit_solution(14734773763532612997)
XLA Ops:
  0.0 2.0 %collective-permute-start = (f32[4,1024]{1,0:T(4,128)}, f32[4,1024]{1,0:T(4,128)S(1)}, u32[]{:S(2)}, u32[]{:S(2)}) collective-permute-start(f32[4,1024]{1,0:T(4,128)} %refs_1_.1), channel_id=1, source_target_pairs={{0,1},{1,0},{2,3},{3,2},{4,5},{5,4},{6,7},{7,6},{8,9},{9,8},{10,11... | collective-permute-start | bytes 49160 | tf_op jit(solution)/shard_map/ppermute | solution.py:187
  2.0 1.9 %prepare.1 = (f32[40,2048]{1,0:T(8,128)S(1)}, f32[4,1024]{1,0:T(4,128)S(1)}, s32[4,2048]{1,0:T(4,128)S(1)}, f32[4,2048]{1,0:T(4,128)S(1)}, f32[48,512]{1,0:T(8,1...) custom-call(f32[40,2048]{1,0:T(8,128)} %bitcast.4, ...), custom_call_target="tpu_custom_call" | custom-call | flops 167772160 | bytes 655360 | tf_op jit(solution)/shard_map/prepare/pallas_call | solution.py:217
  3.9 0.0 collective-permute-done.refs_5_
  3.9 0.3 %send.1 = (f32[48,128]{1,0:T(8,128)S(1)}, f32[48,128]{1,0:T(8,128)S(1)}, f32[48,128]{1,0:T(8,128)S(1)}, f32[48,128]{1,0:T(8,128)S(1)}, f32[4,2048]{1,0:T(4,128)S(1)}) custom-call(f32[48,512]{1,0:T(8,128)S(1)} %get-tuple-element.20.refs_0_, bf16[128,512]{1,0:T(8,128)(2,1)S(1)} %get-tuple-element.21.refs_1_, bf16[128,512]{1,0:T(8,128)(2,1)S(1)} %get-tuple-element.22.refs_2_, ...), custom_call_target="tpu_custom_call" | custom-call | tf_op jit(solution)/shard_map/send/pallas_call | solution.py:244
  4.2 1.3 %collective-permute-start.1 = (f32[48,128]{1,0:T(8,128)S(1)}, f32[48,128]{1,0:T(8,128)S(1)}, u32[]{:S(2)}, u32[]{:S(2)}) collective-permute-start(f32[48,128]{1,0:T(8,128)S(1)} %get-tuple-element.27), channel_id=1, source_target_pairs={{0,8},{2,0},{4,2},{6,4},{8,10},{10,12},{12,14},{14,6},{16,24},{18,... | collective-permute-start | bytes 73736 | tf_op jit(solution)/shard_map/ppermute | solution.py:198
  5.5 1.4 %collective-permute-start.2 = (f32[48,128]{1,0:T(8,128)S(1)}, f32[48,128]{1,0:T(8,128)S(1)}, u32[]{:S(2)}, u32[]{:S(2)}) collective-permute-start(f32[48,128]{1,0:T(8,128)S(1)} %get-tuple-element.28), channel_id=1, source_target_pairs={{0,8},{8,16},{16,24},{24,0},{1,9},{9,17},{17,25},{25,1},{2,10},{10... | collective-permute-start | bytes 73736 | tf_op jit(solution)/shard_map/ppermute | solution.py:187
  6.9 0.0 collective-permute-start.3
  6.9 0.7 %collective-permute-start.4 = (f32[48,128]{1,0:T(8,128)S(1)}, f32[48,128]{1,0:T(8,128)S(1)}, u32[]{:S(2)}, u32[]{:S(2)}) collective-permute-start(f32[48,128]{1,0:T(8,128)S(1)} %get-tuple-element.30), channel_id=1, source_target_pairs={{0,24},{8,0},{16,8},{24,16},{1,25},{9,1},{17,9},{25,17},{2,26},{10... | collective-permute-start | bytes 73736 | tf_op jit(solution)/shard_map/ppermute | solution.py:187
  7.6 2.6 %local.1.acc_ref = f32[640,256]{1,0:T(8,128)S(1)} custom-call(f32[40,2048]{1,0:T(8,128)S(1)} %get-tuple-element.18.refs_0_, s32[4,2048]{1,0:T(4,128)S(1)} %get-tuple-element.19.refs_1_, f32[4,2048]{1,0:T(4,128)S(1)} %get-tuple-element.25.refs_2_, f32[640,256]{1,0:T(8,128)S(1)} %get-tuple-element.26.refs_3_), custom_call_target="tpu_custom_call" | custom-call | flops 2684354560 | bytes 655360 | tf_op jit(solution)/shard_map/local/pallas_call | solution.py:263
  10.2 0.0 collective-permute-done.1.refs_0_
  10.2 0.0 collective-permute-done.2.refs_1_
  10.2 0.0 collective-permute-done.3.refs_2_
  10.2 0.2 %collective-permute-done.4.refs_3_ = f32[48,128]{1,0:T(8,128)S(1)} collective-permute-done((f32[48,128]{1,0:T(8,128)S(1)}, f32[48,128]{1,0:T(8,128)S(1)}, u32[]{:S(2)}, u32[]{:S(2)}) %collective-permute-start.4) | collective-permute-done | bytes 24608 | tf_op jit(solution)/shard_map/ppermute | solution.py:187
  10.4 1.1 %arrive.1 = f32[40,2048]{1,0:T(8,128)} custom-call(f32[640,256]{1,0:T(8,128)S(1)} %local.1.acc_ref, f32[48,128]{1,0:T(8,128)S(1)} %collective-permute-done.1.refs_0_, f32[48,128]{1,0:T(8,128)S(1)} %collective-permute-done.2.refs_1_, f32[48,128]{1,0:T(8,128)S(1)} %collective-permute-done.3.refs_2_, f32[48,128]{1,0:T(8,128)S(1)} %collective-permute-done.4.refs_3_), custom_call_target="tpu_custom_call" | custom-call | tf_op jit(solution)/shard_map/arrive/pallas_call | solution.py:274
Async XLA Ops:
  0.0 3.9 %collective-permute-start = (f32[4,1024]{1,0:T(4,128)}, f32[4,1024]{1,0:T(4,128)S(1)}, u32[]{:S(2)}, u32[]{:S(2)}) collective-permute-start(f32[4,1024]{1,0:T(4,128)} %refs_1_.1), channel_id=1, source_target_pairs={{0,1},{1,0},{2,3},{3,2},{4,5},{5,4},{6,7},{7,6},{8,9},{9,8},{10,11... | collective-permute-start | bytes 49160 | tf_op jit(solution)/shard_map/ppermute | solution.py:187
  4.2 6.0 %collective-permute-start.1 = (f32[48,128]{1,0:T(8,128)S(1)}, f32[48,128]{1,0:T(8,128)S(1)}, u32[]{:S(2)}, u32[]{:S(2)}) collective-permute-start(f32[48,128]{1,0:T(8,128)S(1)} %get-tuple-element.27), channel_id=1, source_target_pairs={{0,8},{2,0},{4,2},{6,4},{8,10},{10,12},{12,14},{14,6},{16,24},{18,... | collective-permute-start | bytes 73736 | tf_op jit(solution)/shard_map/ppermute | solution.py:198
  5.5 4.7 %collective-permute-start.2 = (f32[48,128]{1,0:T(8,128)S(1)}, f32[48,128]{1,0:T(8,128)S(1)}, u32[]{:S(2)}, u32[]{:S(2)}) collective-permute-start(f32[48,128]{1,0:T(8,128)S(1)} %get-tuple-element.28), channel_id=1, source_target_pairs={{0,8},{8,16},{16,24},{24,0},{1,9},{9,17},{17,25},{25,1},{2,10},{10... | collective-permute-start | bytes 73736 | tf_op jit(solution)/shard_map/ppermute | solution.py:187
  6.9 3.3 %collective-permute-start.3 = (f32[48,128]{1,0:T(8,128)S(1)}, f32[48,128]{1,0:T(8,128)S(1)}, u32[]{:S(2)}, u32[]{:S(2)}) collective-permute-start(f32[48,128]{1,0:T(8,128)S(1)} %get-tuple-element.29), channel_id=1, source_target_pairs={{0,2},{2,4},{4,6},{6,14},{8,0},{10,8},{12,10},{14,12},{16,18},{18,... | collective-permute-start | bytes 73736 | tf_op jit(solution)/shard_map/ppermute | solution.py:198
  6.9 3.5 %collective-permute-start.4 = (f32[48,128]{1,0:T(8,128)S(1)}, f32[48,128]{1,0:T(8,128)S(1)}, u32[]{:S(2)}, u32[]{:S(2)}) collective-permute-start(f32[48,128]{1,0:T(8,128)S(1)} %get-tuple-element.30), channel_id=1, source_target_pairs={{0,24},{8,0},{16,8},{24,16},{1,25},{9,1},{17,9},{25,17},{2,26},{10... | collective-permute-start | bytes 73736 | tf_op jit(solution)/shard_map/ppermute | solution.py:187

commit v7 on v6

--- a/solution.py
+++ b/solution.py
@@ -49,7 +49,7 @@
 
 def prepare_kernel(
     levels, early, u_hbm, w_hbm, dep_hbm, sp_hbm, bc_hbm, rot_hbm,
-    u_ref, w_ref, dep_ref, keep_ref, picked_ref, live_ref, lane_ref, acc_ref,
+    u_ref, w_ref, dep_ref, keep_ref, picked_ref, lane_ref, tile_ref, live_ref, acc_ref,
     sp_ref, bc_ref, rot_ref, sems,
 ):
     pairs = [(sp_hbm, sp_ref), (bc_hbm, bc_ref), (rot_hbm, rot_ref), (dep_hbm, dep_ref), (u_hbm, u_ref), (w_hbm, w_ref)]
@@ -71,12 +71,14 @@
         tile = column // LANES
         which.append(k)
         columns.append(column)
-        codes.append(jnp.where(slot < bc_ref[0:1, j : j + 1], tile * SUB + k, -1))
+        alive = slot < bc_ref[0:1, j : j + 1]
+        codes.append(jnp.where(alive, tile * SUB + k, -1))
         lanes.append(column - tile * LANES)
+        lane_ref[j : j + 1, :] = lanes[j]
+        tile_ref[j : j + 1, :] = tile
+        live_ref[j : j + 1, :] = jnp.where(alive, k, -1)
     live = one_hot(tiles * SUB, jnp.concatenate(codes, axis=1))
     lane = one_hot(LANES, jnp.concatenate(lanes, axis=1))
-    live_ref[...] = live
-    lane_ref[...] = lane
     sent = lax.dot_general(live, lane, NT, preferred_element_type=F32)
     for t in range(tiles):
         keep_ref[:, t * LANES : (t + 1) * LANES] = 1.0 - sent[t * SUB : t * SUB + stencil]
@@ -126,48 +128,42 @@
     )
 
 
-def send_kernel(count, paired, picked_ref, live_ref, lane_ref, keep_ref, *refs):
-    parts, outs, masked_ref, full = refs[:count], refs[count:-2], refs[-2], refs[-1]
+def send_kernel(count, paired, picked_ref, lane_ref, tile_ref, live_ref, *refs):
+    parts, outs, full = refs[:count], refs[count:-1], refs[-1]
     stencil, cells = full.shape
     rows = picked_ref.shape[0] - SUB
-    blocks, slots = len(outs), outs[0].shape[1]
+    blocks, slots = lane_ref.shape
     for steps, part in enumerate(parts):
         full[:, piece(steps, part.shape[1])] = part[...]
     pad = jnp.zeros((SUB - stencil, LANES), F32)
-    pieces = []
-    for t in range(cells // LANES):
-        pieces += [full[:, t * LANES : (t + 1) * LANES], pad]
-    w = jnp.concatenate(pieces, axis=0)
-    w0 = w.astype(BF16).astype(F32)
-    w1 = (w - w0).astype(BF16).astype(F32)
-    terms = jnp.concatenate([w0, w1, w - w0 - w1], axis=0).astype(BF16)
-    got = jnp.dot(terms, lane_ref[...], preferred_element_type=F32)
-    n = w.shape[0]
-    got = (got[:n] + got[n : 2 * n] + got[2 * n :]) * live_ref[...].astype(F32)
-    weight = jnp.sum(got, axis=0, keepdims=True)
-    message = [
-        jnp.concatenate(
-            [picked_ref[:rows, j * slots : (j + 1) * slots] * weight[:, j * slots : (j + 1) * slots], picked_ref[rows:, j * slots : (j + 1) * slots]],
-            axis=0,
-        )
-        for j in range(blocks)
+    table = [
+        jnp.concatenate([full[:, t * LANES : (t + 1) * LANES], pad], axis=0) for t in range(cells // LANES)
     ]
+    row = lax.broadcasted_iota(I32, (SUB, slots), 0)
+    message = []
+    for j in range(blocks):
+        lane = jnp.broadcast_to(lane_ref[j : j + 1, :], (SUB, slots))
+        tile = jnp.broadcast_to(tile_ref[j : j + 1, :], (SUB, slots))
+        found = jnp.zeros((SUB, slots), F32)
+        for t, piece_t in enumerate(table):
+            found = jnp.where(tile == t, jnp.take_along_axis(piece_t, lane, axis=1, mode="promise_in_bounds"), found)
+        weight = jnp.sum(jnp.where(row == live_ref[j : j + 1, :], found, 0.0), axis=0, keepdims=True)
+        here = slice(j * slots, (j + 1) * slots)
+        message.append(jnp.concatenate([picked_ref[:rows, here] * weight, picked_ref[rows:, here]], axis=0))
     low, high, previous, following = message
     if paired:
         even = lax.rem(lax.axis_index("panel"), 2) == 0
         low, high = jnp.where(even, low, high), jnp.where(even, high, low)
-    message = [low, following, high, previous]
-    for out, m in zip(outs, message):
+    for out, m in zip(outs, [low, following, high, previous]):
         out[...] = m
-    masked_ref[...] = full[...] * keep_ref[...]
-
-
-def local_kernel(early, count, u_ref, dep_ref, w_ref, early_ref, acc_ref):
+
+
+def local_kernel(early, count, u_ref, dep_ref, w_ref, keep_ref, early_ref, acc_ref):
     stencil, cells = dep_ref.shape
     at = [(k, piece(s, cells // count)) for k in range(early) for s in range(1, count)]
     at += [(k, slice(None)) for k in range(early, stencil)]
     acc_ref[...] = early_ref[...] + scatter_product(
-        [scattered(u_ref, dep_ref, w_ref[k : k + 1, here], k, here) for k, here in at], cells
+        [scattered(u_ref, dep_ref, w_ref[k : k + 1, here] * keep_ref[k : k + 1, here], k, here) for k, here in at], cells
     )
 
 
@@ -214,7 +210,7 @@
         block_count.reshape(1, -1), rotation.reshape(1, -1),
     )
     sums = shape((cells // LO * 2 * rows, LO), F32)
-    u, own, dep, keep, picked, live, lane, acc = pl.pallas_call(
+    u, own, dep, keep, picked, *slot_rows, acc = pl.pallas_call(
         lambda *refs: prepare_kernel(levels, early, *refs),
         out_shape=[
             shape((rows, cells), F32),
@@ -222,12 +218,11 @@
             shape((stencil, cells), I32),
             shape((stencil, cells), F32),
             shape((rows + SUB, points), F32),
-            shape((cells // LANES * SUB, points), BF16),
-            shape((LANES, points), BF16),
+            *([shape((blocks, slots), I32)] * 3),
             sums,
         ],
         in_specs=[HBM] * 6,
-        out_specs=[VMEM] * 8,
+        out_specs=[VMEM] * 9,
         scratch_shapes=[
             pltpu.VMEM((blocks, slots), I32),
             pltpu.VMEM((1, block_count.size), I32),
@@ -241,15 +236,14 @@
         name="prepare",
     )(*(pltpu.with_memory_space_constraint(a, pltpu.HBM) for a in inputs))
     block = shape((rows + SUB, slots), F32)
-    *outgoing, masked = pl.pallas_call(
+    *outgoing, full = pl.pallas_call(
         lambda *refs: send_kernel(count, paired, *refs),
         out_shape=[block] * blocks + [shape((stencil, cells), F32)],
         in_specs=[VMEM] * (4 + count),
         out_specs=[VMEM] * (blocks + 1),
-        scratch_shapes=[pltpu.VMEM((stencil, cells), F32)],
         compiler_params=PARAMS,
         name="send",
-    )(picked, live, lane, keep, own, *parts)
+    )(picked, *slot_rows, own, *parts)
     if paired:
         back, forth = (lambda v: racetrack(v, True)), (lambda v: racetrack(v, False))
     else:
@@ -263,14 +257,14 @@
     local = pl.pallas_call(
         lambda *refs: local_kernel(early, count, *refs),
         out_shape=sums,
-        in_specs=[VMEM] * 4,
+        in_specs=[VMEM] * 5,
         out_specs=VMEM,
         cost_estimate=pl.CostEstimate(
             flops=4 * rows * cells * stencil * cells, bytes_accessed=8 * rows * cells, transcendentals=0
         ),
         compiler_params=PARAMS,
         name="local",
-    )(u, dep, masked, acc)
+    )(u, dep, full, keep, acc)
     out = pl.pallas_call(
         arrive_kernel,
         out_shape=shape((rows, cells), F32),

time: 11.7 us -> 11.6 us (level)
  no operation moved by 1% of the time
where the time goes in v7:
time: 11.6 us; the launch traced here: 11.4 us
  Pallas kernels  5.76 us (50%)
  starting transfers between devices  5.43 us (47%)
  waiting for transfers between devices  0.19 us (2%)
    ppermute x3, starting transfers between devices, rotated(): lax.ppermute(value, axis, [(i, (i + steps) % count) for i in range(count)])  4.11 us
    pallas_call x1, Pallas kernels, body(): pl.pallas_call(lambda *refs: local_kernel(early, count, *refs), out_shape...  2.58 us
    pallas_call x1, Pallas kernels, body(): pl.pallas_call(lambda *refs: prepare_kernel(levels, early, *refs), out_sh...  1.87 us
    ppermute x2, starting transfers between devices, racetrack(): return lax.ppermute(value, ('panel', 'tile'), route)  1.31 us
    pallas_call x1, Pallas kernels, body(): pl.pallas_call(arrive_kernel, out_shape=shape((rows, cells), F32), in_spe...  1.14 us
  transfers between devices with their start and end apart: 5, of which 1 were waited for; matrix products, arithmetic and copies ran while one was open for 0% of the time, Pallas kernels for 39%

profile of v7, /device:TPU:1, one launch (start us, length us, event | category | flops | bytes accessed | tf_op | source)
XLA Modules:
  0.0 11.4 jit_solution(15641091299243929540)
XLA Ops:
  0.0 2.0 %collective-permute-start = (f32[4,1024]{1,0:T(4,128)}, f32[4,1024]{1,0:T(4,128)S(1)}, u32[]{:S(2)}, u32[]{:S(2)}) collective-permute-start(f32[4,1024]{1,0:T(4,128)} %refs_1_.1), channel_id=1, source_target_pairs={{0,1},{1,0},{2,3},{3,2},{4,5},{5,4},{6,7},{7,6},{8,9},{9,8},{10,11... | collective-permute-start | bytes 49160 | tf_op jit(solution)/shard_map/ppermute | solution.py:183
  2.0 1.9 %prepare.1 = (f32[40,2048]{1,0:T(8,128)S(1)}, f32[4,1024]{1,0:T(4,128)S(1)}, s32[4,2048]{1,0:T(4,128)S(1)}, f32[4,2048]{1,0:T(4,128)S(1)}, f32[48,512]{1,0:T(8,1...) custom-call(f32[40,2048]{1,0:T(8,128)} %bitcast.4, ...), custom_call_target="tpu_custom_call" | custom-call | flops 167772160 | bytes 655360 | tf_op jit(solution)/shard_map/prepare/pallas_call | solution.py:213
  3.9 0.0 collective-permute-done.refs_5_
  3.9 0.2 %send.1 = (f32[48,128]{1,0:T(8,128)S(1)}, f32[48,128]{1,0:T(8,128)S(1)}, f32[48,128]{1,0:T(8,128)S(1)}, f32[48,128]{1,0:T(8,128)S(1)}, f32[4,2048]{1,0:T(4,128)S(1)}) custom-call(f32[48,512]{1,0:T(8,128)S(1)} %get-tuple-element.21.refs_0_, s32[4,128]{1,0:T(4,128)S(1)} %get-tuple-element.22.refs_1_, s32[4,128]{1,0:T(4,128)S(1)} %get-tuple-element.23.refs_2_, ...), custom_call_target="tpu_custom_call" | custom-call | tf_op jit(solution)/shard_map/send/pallas_call | solution.py:239
  4.1 1.3 %collective-permute-start.1 = (f32[48,128]{1,0:T(8,128)S(1)}, f32[48,128]{1,0:T(8,128)S(1)}, u32[]{:S(2)}, u32[]{:S(2)}) collective-permute-start(f32[48,128]{1,0:T(8,128)S(1)} %get-tuple-element.29), channel_id=1, source_target_pairs={{0,8},{2,0},{4,2},{6,4},{8,10},{10,12},{12,14},{14,6},{16,24},{18,... | collective-permute-start | bytes 73736 | tf_op jit(solution)/shard_map/ppermute | solution.py:194
  5.4 1.4 %collective-permute-start.2 = (f32[48,128]{1,0:T(8,128)S(1)}, f32[48,128]{1,0:T(8,128)S(1)}, u32[]{:S(2)}, u32[]{:S(2)}) collective-permute-start(f32[48,128]{1,0:T(8,128)S(1)} %get-tuple-element.30), channel_id=1, source_target_pairs={{0,8},{8,16},{16,24},{24,0},{1,9},{9,17},{17,25},{25,1},{2,10},{10... | collective-permute-start | bytes 73736 | tf_op jit(solution)/shard_map/ppermute | solution.py:183
  6.8 0.0 collective-permute-start.3
  6.8 0.7 %collective-permute-start.4 = (f32[48,128]{1,0:T(8,128)S(1)}, f32[48,128]{1,0:T(8,128)S(1)}, u32[]{:S(2)}, u32[]{:S(2)}) collective-permute-start(f32[48,128]{1,0:T(8,128)S(1)} %get-tuple-element.32), channel_id=1, source_target_pairs={{0,24},{8,0},{16,8},{24,16},{1,25},{9,1},{17,9},{25,17},{2,26},{10... | collective-permute-start | bytes 73736 | tf_op jit(solution)/shard_map/ppermute | solution.py:183
  7.5 2.6 %local.1.acc_ref = f32[640,256]{1,0:T(8,128)S(1)} custom-call(f32[40,2048]{1,0:T(8,128)S(1)} %get-tuple-element.19.refs_0_, s32[4,2048]{1,0:T(4,128)S(1)} %get-tuple-element.20.refs_1_, f32[4,2048]{1,0:T(4,128)S(1)} %get-tuple-element.26.refs_2_, f32[4,2048]{1,0:T(4,128)S(1)} %get-tuple-element.27.refs_3_, f32[640,256]{1,0:T(8,128)S(1)} %get-tuple-element.28.refs_4_), custom_call_target="tpu_custom_call" | custom-call | flops 2684354560 | bytes 655360 | tf_op jit(solution)/shard_map/local/pallas_call | solution.py:257
  10.1 0.0 collective-permute-done.1.refs_0_
  10.1 0.0 collective-permute-done.2.refs_1_
  10.1 0.0 collective-permute-done.3.refs_2_
  10.1 0.2 %collective-permute-done.4.refs_3_ = f32[48,128]{1,0:T(8,128)S(1)} collective-permute-done((f32[48,128]{1,0:T(8,128)S(1)}, f32[48,128]{1,0:T(8,128)S(1)}, u32[]{:S(2)}, u32[]{:S(2)}) %collective-permute-start.4) | collective-permute-done | bytes 24608 | tf_op jit(solution)/shard_map/ppermute | solution.py:183
  10.3 1.1 %arrive.1 = f32[40,2048]{1,0:T(8,128)} custom-call(f32[640,256]{1,0:T(8,128)S(1)} %local.1.acc_ref, f32[48,128]{1,0:T(8,128)S(1)} %collective-permute-done.1.refs_0_, f32[48,128]{1,0:T(8,128)S(1)} %collective-permute-done.2.refs_1_, f32[48,128]{1,0:T(8,128)S(1)} %collective-permute-done.3.refs_2_, f32[48,128]{1,0:T(8,128)S(1)} %collective-permute-done.4.refs_3_), custom_call_target="tpu_custom_call" | custom-call | tf_op jit(solution)/shard_map/arrive/pallas_call | solution.py:268
Async XLA Ops:
  0.0 3.9 %collective-permute-start = (f32[4,1024]{1,0:T(4,128)}, f32[4,1024]{1,0:T(4,128)S(1)}, u32[]{:S(2)}, u32[]{:S(2)}) collective-permute-start(f32[4,1024]{1,0:T(4,128)} %refs_1_.1), channel_id=1, source_target_pairs={{0,1},{1,0},{2,3},{3,2},{4,5},{5,4},{6,7},{7,6},{8,9},{9,8},{10,11... | collective-permute-start | bytes 49160 | tf_op jit(solution)/shard_map/ppermute | solution.py:183
  4.1 6.0 %collective-permute-start.1 = (f32[48,128]{1,0:T(8,128)S(1)}, f32[48,128]{1,0:T(8,128)S(1)}, u32[]{:S(2)}, u32[]{:S(2)}) collective-permute-start(f32[48,128]{1,0:T(8,128)S(1)} %get-tuple-element.29), channel_id=1, source_target_pairs={{0,8},{2,0},{4,2},{6,4},{8,10},{10,12},{12,14},{14,6},{16,24},{18,... | collective-permute-start | bytes 73736 | tf_op jit(solution)/shard_map/ppermute | solution.py:194
  5.4 4.7 %collective-permute-start.2 = (f32[48,128]{1,0:T(8,128)S(1)}, f32[48,128]{1,0:T(8,128)S(1)}, u32[]{:S(2)}, u32[]{:S(2)}) collective-permute-start(f32[48,128]{1,0:T(8,128)S(1)} %get-tuple-element.30), channel_id=1, source_target_pairs={{0,8},{8,16},{16,24},{24,0},{1,9},{9,17},{17,25},{25,1},{2,10},{10... | collective-permute-start | bytes 73736 | tf_op jit(solution)/shard_map/ppermute | solution.py:183
  6.8 3.3 %collective-permute-start.3 = (f32[48,128]{1,0:T(8,128)S(1)}, f32[48,128]{1,0:T(8,128)S(1)}, u32[]{:S(2)}, u32[]{:S(2)}) collective-permute-start(f32[48,128]{1,0:T(8,128)S(1)} %get-tuple-element.31), channel_id=1, source_target_pairs={{0,2},{2,4},{4,6},{6,14},{8,0},{10,8},{12,10},{14,12},{16,18},{18,... | collective-permute-start | bytes 73736 | tf_op jit(solution)/shard_map/ppermute | solution.py:194
  6.8 3.5 %collective-permute-start.4 = (f32[48,128]{1,0:T(8,128)S(1)}, f32[48,128]{1,0:T(8,128)S(1)}, u32[]{:S(2)}, u32[]{:S(2)}) collective-permute-start(f32[48,128]{1,0:T(8,128)S(1)} %get-tuple-element.32), channel_id=1, source_target_pairs={{0,24},{8,0},{16,8},{24,16},{1,25},{9,1},{17,9},{25,17},{2,26},{10... | collective-permute-start | bytes 73736 | tf_op jit(solution)/shard_map/ppermute | solution.py:183

commit v8 on v7

--- a/solution.py
+++ b/solution.py
@@ -45,6 +45,13 @@
 
 def scattered(u_ref, dep_ref, weight, k, at):
     return two_terms(u_ref[:, at] * weight).astype(BF16), dep_ref[k : k + 1, at]
+
+
+def picked_lanes(tiles, lane, tile):
+    found = jnp.zeros(lane.shape, F32)
+    for t, table in enumerate(tiles):
+        found = jnp.where(tile == t, jnp.take_along_axis(table, lane, axis=1, mode="promise_in_bounds"), found)
+    return found
 
 
 def prepare_kernel(
@@ -63,14 +70,13 @@
     blocks, slots = sp_ref.shape
     tiles = cells // LANES
     slot = lax.broadcasted_iota(I32, (1, slots), 1)
-    which, columns, codes, lanes = [], [], [], []
+    which, codes, lanes = [], [], []
     for j in range(blocks):
         chosen = sp_ref[j : j + 1, :]
         k = chosen // cells
         column = chosen - k * cells
         tile = column // LANES
         which.append(k)
-        columns.append(column)
         alive = slot < bc_ref[0:1, j : j + 1]
         codes.append(jnp.where(alive, tile * SUB + k, -1))
         lanes.append(column - tile * LANES)
@@ -84,37 +90,19 @@
         keep_ref[:, t * LANES : (t + 1) * LANES] = 1.0 - sent[t * SUB : t * SUB + stencil]
     for c in copies[3:]:
         c.wait()
-    dep = dep_ref[...]
-    dep_high = dep // SUB
-    dep_low = dep - dep_high * SUB
-    table = jnp.concatenate(
-        [two_terms(u_ref[...]), dep_high.astype(F32), dep_low.astype(F32), jnp.zeros((SUB, cells), F32)],
-        axis=0,
-    ).astype(BF16)
-    column = jnp.concatenate(columns, axis=1)
-    chunk = column // LO
-    height = table.shape[0]
-    got = jnp.dot(
-        jnp.concatenate([table[:, c * LO : (c + 1) * LO] for c in range(cells // LO)], axis=0),
-        one_hot(LO, column - chunk * LO),
-        preferred_element_type=F32,
-    )
-    values = jnp.zeros((rows, blocks * slots), F32)
-    targets = jnp.zeros((2 * stencil, blocks * slots), F32)
-    for c in range(cells // LO):
-        at = c * height
-        here = chunk == c
-        values = values + jnp.where(here, got[at : at + rows] + got[at + rows : at + 2 * rows], 0.0)
-        targets = targets + jnp.where(here, got[at + 2 * rows : at + 2 * rows + 2 * stencil], 0.0)
-    k = jnp.concatenate(which, axis=1)
-    ids = jnp.zeros((1, blocks * slots), F32)
-    for i in range(stencil):
-        ids = ids + jnp.where(k == i, targets[i : i + 1] * SUB + targets[stencil + i : stencil + i + 1], 0.0)
-    picked_ref[rows:, :] = jnp.broadcast_to(ids, (SUB, blocks * slots))
-    picked_ref[2 * levels : rows, :] = values[2 * levels :]
+    pad = jnp.zeros((SUB - stencil, LANES), F32)
+    spans = [slice(t * LANES, (t + 1) * LANES) for t in range(tiles)]
+    targets = [jnp.concatenate([dep_ref[:, span].astype(F32), pad], axis=0) for span in spans]
+    row = lax.broadcasted_iota(I32, (SUB, slots), 0)
     for j in range(blocks):
         here = slice(j * slots, (j + 1) * slots)
-        zonal, merid = values[:levels, here], values[levels : 2 * levels, here]
+        at = jnp.broadcast_to(lane_ref[j : j + 1, :], (SUB, slots)), jnp.broadcast_to(tile_ref[j : j + 1, :], (SUB, slots))
+        ids = jnp.where(row == which[j], picked_lanes(targets, *at), 0.0)
+        picked_ref[rows:, here] = jnp.broadcast_to(jnp.sum(ids, axis=0, keepdims=True), (SUB, slots))
+        values = jnp.concatenate(
+            [picked_lanes([u_ref[g : g + SUB, span] for span in spans], *at) for g in range(0, rows, SUB)], axis=0
+        )
+        zonal, merid = values[:levels], values[levels : 2 * levels]
         if j >= 2:
             code = rot_ref[0:1, j - 2 : j - 1]
             cosine = (code == 0).astype(F32) - (code == 2).astype(F32)
@@ -122,6 +110,7 @@
             zonal, merid = cosine * zonal + sine * merid, cosine * merid - sine * zonal
         picked_ref[:levels, here] = zonal
         picked_ref[levels : 2 * levels, here] = merid
+        picked_ref[2 * levels : rows, here] = values[2 * levels :]
     own = piece(0, w_ref.shape[1])
     acc_ref[...] = scatter_product(
         [scattered(u_ref, dep_ref, w_ref[k : k + 1, :] * keep_ref[k : k + 1, own], k, own) for k in range(early)], cells
@@ -144,9 +133,7 @@
     for j in range(blocks):
         lane = jnp.broadcast_to(lane_ref[j : j + 1, :], (SUB, slots))
         tile = jnp.broadcast_to(tile_ref[j : j + 1, :], (SUB, slots))
-        found = jnp.zeros((SUB, slots), F32)
-        for t, piece_t in enumerate(table):
-            found = jnp.where(tile == t, jnp.take_along_axis(piece_t, lane, axis=1, mode="promise_in_bounds"), found)
+        found = picked_lanes(table, lane, tile)
         weight = jnp.sum(jnp.where(row == live_ref[j : j + 1, :], found, 0.0), axis=0, keepdims=True)
         here = slice(j * slots, (j + 1) * slots)
         message.append(jnp.concatenate([picked_ref[:rows, here] * weight, picked_ref[rows:, here]], axis=0))
@@ -167,15 +154,30 @@
     )
 
 
-def arrive_kernel(acc_ref, *refs):
-    received, out_ref = refs[:-1], refs[-1]
-    rows, cells = out_ref.shape
+def arrived_sums(received, cells):
+    rows = received[0].shape[0] - SUB
     values = jnp.concatenate([r[:rows, :] for r in received], axis=1)
     ids = jnp.concatenate([r[rows : rows + 1, :] for r in received], axis=1).astype(I32)
     sums = scatter_product([(two_terms(values).astype(BF16), ids)], cells)
-    for h in range(cells // LO):
+    return [
+        sums[2 * h * rows : (2 * h + 1) * rows] + sums[(2 * h + 1) * rows : (2 * h + 2) * rows]
+        for h in range(cells // LO)
+    ]
+
+
+def merge_kernel(acc_ref, *refs):
+    received, out_ref = refs[:-1], refs[-1]
+    rows, cells = out_ref.shape
+    for h, sums in enumerate(arrived_sums(received, cells)):
         a, b, c = (2 * h * rows + i * rows for i in range(3))
-        out_ref[:, h * LO : (h + 1) * LO] = (acc_ref[a:b] + acc_ref[b:c]) + (sums[a:b] + sums[b:c])
+        out_ref[:, h * LO : (h + 1) * LO] = (acc_ref[a:b] + acc_ref[b:c]) + sums
+
+
+def arrive_kernel(merged_ref, *refs):
+    received, out_ref = refs[:-1], refs[-1]
+    for h, sums in enumerate(arrived_sums(received, out_ref.shape[1])):
+        here = slice(h * LO, (h + 1) * LO)
+        out_ref[:, here] = merged_ref[:, here] + sums
 
 
 def rotated(value, axis, steps):
@@ -254,7 +256,7 @@
         forth(outgoing[2]),
         rotated(outgoing[3], "panel", -1),
     ]
-    local = pl.pallas_call(
+    acc = pl.pallas_call(
         lambda *refs: local_kernel(early, count, *refs),
         out_shape=sums,
         in_specs=[VMEM] * 5,
@@ -265,14 +267,26 @@
         compiler_params=PARAMS,
         name="local",
     )(u, dep, full, keep, acc)
+    result = shape((rows, cells), F32)
+    merged = pl.pallas_call(
+        merge_kernel,
+        out_shape=result,
+        in_specs=[VMEM] * blocks,
+        out_specs=VMEM,
+        cost_estimate=pl.CostEstimate(
+            flops=4 * rows * cells * points, bytes_accessed=8 * rows * cells, transcendentals=0
+        ),
+        compiler_params=PARAMS,
+        name="merge",
+    )(acc, *received[:-1])
     out = pl.pallas_call(
         arrive_kernel,
-        out_shape=shape((rows, cells), F32),
-        in_specs=[VMEM] * (1 + blocks),
+        out_shape=result,
+        in_specs=[VMEM] * 2,
         out_specs=VMEM,
         compiler_params=PARAMS,
         name="arrive",
-    )(local, *received)
+    )(merged, received[-1])
     return out.reshape(fields, levels, cells)
 
 

time: 11.6 us -> 11.5 us (level)
  the two profiles are of different devices: /device:TPU:1 before, /device:TPU:0 now
where the time goes in v8:
time: 11.5 us; the launch traced here: 11.4 us
  Pallas kernels  5.79 us (50%)
  starting transfers between devices  5.25 us (46%)
  waiting for transfers between devices  0.23 us (2%)
    ppermute x3, starting transfers between devices, rotated(): lax.ppermute(value, axis, [(i, (i + steps) % count) for i in range(count)])  3.65 us
    pallas_call x1, Pallas kernels, body(): pl.pallas_call(lambda *refs: local_kernel(early, count, *refs), out_shape...  2.58 us
    pallas_call x1, Pallas kernels, body(): pl.pallas_call(lambda *refs: prepare_kernel(levels, early, *refs), out_sh...  1.7 us
    ppermute x2, starting transfers between devices, racetrack(): return lax.ppermute(value, ('panel', 'tile'), route)  1.6 us
    pallas_call x1, Pallas kernels, body(): pl.pallas_call(arrive_kernel, out_shape=result, in_specs=[VMEM] * 2, out_...  0.98 us
    pallas_call x1, Pallas kernels, body(): pl.pallas_call(merge_kernel, out_shape=result, in_specs=[VMEM] * blocks,...  0.37 us
  transfers between devices with their start and end apart: 5, of which 1 were waited for; matrix products, arithmetic and copies ran while one was open for 0% of the time, Pallas kernels for 41%

profile of v8, /device:TPU:0, one launch (start us, length us, event | category | flops | bytes accessed | tf_op | source)
XLA Modules:
  0.0 11.4 jit_solution(14392525957826837932)
XLA Ops:
  0.0 3.0 %collective-permute-start = (f32[4,1024]{1,0:T(4,128)}, f32[4,1024]{1,0:T(4,128)S(1)}, u32[]{:S(2)}, u32[]{:S(2)}) collective-permute-start(f32[4,1024]{1,0:T(4,128)} %refs_1_.1), channel_id=1, source_target_pairs={{0,1},{1,0},{2,3},{3,2},{4,5},{5,4},{6,7},{7,6},{8,9},{9,8},{10,11... | collective-permute-start | bytes 49160 | tf_op jit(solution)/shard_map/ppermute | solution.py:185
  3.0 1.7 %prepare.1 = (f32[40,2048]{1,0:T(8,128)S(1)}, f32[4,1024]{1,0:T(4,128)S(1)}, s32[4,2048]{1,0:T(4,128)S(1)}, f32[4,2048]{1,0:T(4,128)S(1)}, f32[48,512]{1,0:T(8,1...) custom-call(f32[40,2048]{1,0:T(8,128)} %bitcast.4, ...), custom_call_target="tpu_custom_call" | custom-call | flops 167772160 | bytes 655360 | tf_op jit(solution)/shard_map/prepare/pallas_call | solution.py:215
  4.7 0.2 %collective-permute-done.refs_5_ = f32[4,1024]{1,0:T(4,128)S(1)} collective-permute-done((f32[4,1024]{1,0:T(4,128)}, f32[4,1024]{1,0:T(4,128)S(1)}, u32[]{:S(2)}, u32[]{:S(2)}) %collective-permute-start) | collective-permute-done | bytes 16416 | tf_op jit(solution)/shard_map/ppermute | solution.py:185
  4.9 0.2 %send.1 = (f32[48,128]{1,0:T(8,128)S(1)}, f32[48,128]{1,0:T(8,128)S(1)}, f32[48,128]{1,0:T(8,128)S(1)}, f32[48,128]{1,0:T(8,128)S(1)}, f32[4,2048]{1,0:T(4,128)S(1)}) custom-call(f32[48,512]{1,0:T(8,128)S(1)} %get-tuple-element.21.refs_0_, s32[4,128]{1,0:T(4,128)S(1)} %get-tuple-element.22.refs_1_, s32[4,128]{1,0:T(4,128)S(1)} %get-tuple-element.23.refs_2_, ...), custom_call_target="tpu_custom_call" | custom-call | tf_op jit(solution)/shard_map/send/pallas_call | solution.py:241
  5.1 0.0 collective-permute-start.1
  5.1 0.6 %collective-permute-start.2 = (f32[48,128]{1,0:T(8,128)S(1)}, f32[48,128]{1,0:T(8,128)S(1)}, u32[]{:S(2)}, u32[]{:S(2)}) collective-permute-start(f32[48,128]{1,0:T(8,128)S(1)} %get-tuple-element.30), channel_id=1, source_target_pairs={{0,8},{8,16},{16,24},{24,0},{1,9},{9,17},{17,25},{25,1},{2,10},{10... | collective-permute-start | bytes 73736 | tf_op jit(solution)/shard_map/ppermute | solution.py:185
  5.7 1.6 %collective-permute-start.3 = (f32[48,128]{1,0:T(8,128)S(1)}, f32[48,128]{1,0:T(8,128)S(1)}, u32[]{:S(2)}, u32[]{:S(2)}) collective-permute-start(f32[48,128]{1,0:T(8,128)S(1)} %get-tuple-element.31), channel_id=1, source_target_pairs={{0,2},{2,4},{4,6},{6,14},{8,0},{10,8},{12,10},{14,12},{16,18},{18,... | collective-permute-start | bytes 73736 | tf_op jit(solution)/shard_map/ppermute | solution.py:196
  7.3 0.1 collective-permute-start.4
  7.4 2.6 %local.1.acc_ref = f32[640,256]{1,0:T(8,128)S(1)} custom-call(f32[40,2048]{1,0:T(8,128)S(1)} %get-tuple-element.19.refs_0_, s32[4,2048]{1,0:T(4,128)S(1)} %get-tuple-element.20.refs_1_, f32[4,2048]{1,0:T(4,128)S(1)} %get-tuple-element.26.refs_2_, f32[4,2048]{1,0:T(4,128)S(1)} %get-tuple-element.27.refs_3_, f32[640,256]{1,0:T(8,128)S(1)} %get-tuple-element.28.refs_4_), custom_call_target="tpu_custom_call" | custom-call | flops 2684354560 | bytes 655360 | tf_op jit(solution)/shard_map/local/pallas_call | solution.py:259
  9.9 0.0 collective-permute-done.1.refs_0_
  10.0 0.0 collective-permute-done.2.refs_1_
  10.0 0.0 collective-permute-done.3.refs_2_
  10.0 0.4 %merge.1.merged_ref = f32[40,2048]{1,0:T(8,128)S(1)} custom-call(f32[640,256]{1,0:T(8,128)S(1)} %local.1.acc_ref, f32[48,128]{1,0:T(8,128)S(1)} %collective-permute-done.1.refs_0_, f32[48,128]{1,0:T(8,128)S(1)} %collective-permute-done.2.refs_1_, f32[48,128]{1,0:T(8,128)S(1)} %collective-permute-done.3.refs_2_), custom_call_target="tpu_custom_call" | custom-call | flops 167772160 | bytes 655360 | tf_op jit(solution)/shard_map/merge/pallas_call | solution.py:271
  10.4 0.0 collective-permute-done.4.refs_0_
  10.4 1.0 %arrive.1 = f32[40,2048]{1,0:T(8,128)} custom-call(f32[40,2048]{1,0:T(8,128)S(1)} %merge.1.merged_ref, f32[48,128]{1,0:T(8,128)S(1)} %collective-permute-done.4.refs_0_), custom_call_target="tpu_custom_call" | custom-call | tf_op jit(solution)/shard_map/arrive/pallas_call | solution.py:282
Async XLA Ops:
  0.0 4.9 %collective-permute-start = (f32[4,1024]{1,0:T(4,128)}, f32[4,1024]{1,0:T(4,128)S(1)}, u32[]{:S(2)}, u32[]{:S(2)}) collective-permute-start(f32[4,1024]{1,0:T(4,128)} %refs_1_.1), channel_id=1, source_target_pairs={{0,1},{1,0},{2,3},{3,2},{4,5},{5,4},{6,7},{7,6},{8,9},{9,8},{10,11... | collective-permute-start | bytes 49160 | tf_op jit(solution)/shard_map/ppermute | solution.py:185
  5.1 4.9 %collective-permute-start.1 = (f32[48,128]{1,0:T(8,128)S(1)}, f32[48,128]{1,0:T(8,128)S(1)}, u32[]{:S(2)}, u32[]{:S(2)}) collective-permute-start(f32[48,128]{1,0:T(8,128)S(1)} %get-tuple-element.29), channel_id=1, source_target_pairs={{0,8},{2,0},{4,2},{6,4},{8,10},{10,12},{12,14},{14,6},{16,24},{18,... | collective-permute-start | bytes 73736 | tf_op jit(solution)/shard_map/ppermute | solution.py:196
  5.1 4.9 %collective-permute-start.2 = (f32[48,128]{1,0:T(8,128)S(1)}, f32[48,128]{1,0:T(8,128)S(1)}, u32[]{:S(2)}, u32[]{:S(2)}) collective-permute-start(f32[48,128]{1,0:T(8,128)S(1)} %get-tuple-element.30), channel_id=1, source_target_pairs={{0,8},{8,16},{16,24},{24,0},{1,9},{9,17},{17,25},{25,1},{2,10},{10... | collective-permute-start | bytes 73736 | tf_op jit(solution)/shard_map/ppermute | solution.py:185
  5.7 4.2 %collective-permute-start.3 = (f32[48,128]{1,0:T(8,128)S(1)}, f32[48,128]{1,0:T(8,128)S(1)}, u32[]{:S(2)}, u32[]{:S(2)}) collective-permute-start(f32[48,128]{1,0:T(8,128)S(1)} %get-tuple-element.31), channel_id=1, source_target_pairs={{0,2},{2,4},{4,6},{6,14},{8,0},{10,8},{12,10},{14,12},{16,18},{18,... | collective-permute-start | bytes 73736 | tf_op jit(solution)/shard_map/ppermute | solution.py:196
  7.3 3.1 %collective-permute-start.4 = (f32[48,128]{1,0:T(8,128)S(1)}, f32[48,128]{1,0:T(8,128)S(1)}, u32[]{:S(2)}, u32[]{:S(2)}) collective-permute-start(f32[48,128]{1,0:T(8,128)S(1)} %get-tuple-element.32), channel_id=1, source_target_pairs={{0,24},{8,0},{16,8},{24,16},{1,25},{9,1},{17,9},{25,17},{2,26},{10... | collective-permute-start | bytes 73736 | tf_op jit(solution)/shard_map/ppermute | solution.py:185

commit v9 on v8

--- a/solution.py
+++ b/solution.py
@@ -154,30 +154,15 @@
     )
 
 
-def arrived_sums(received, cells):
-    rows = received[0].shape[0] - SUB
+def arrive_kernel(acc_ref, *refs):
+    received, out_ref = refs[:-1], refs[-1]
+    rows, cells = out_ref.shape
     values = jnp.concatenate([r[:rows, :] for r in received], axis=1)
     ids = jnp.concatenate([r[rows : rows + 1, :] for r in received], axis=1).astype(I32)
     sums = scatter_product([(two_terms(values).astype(BF16), ids)], cells)
-    return [
-        sums[2 * h * rows : (2 * h + 1) * rows] + sums[(2 * h + 1) * rows : (2 * h + 2) * rows]
-        for h in range(cells // LO)
-    ]
-
-
-def merge_kernel(acc_ref, *refs):
-    received, out_ref = refs[:-1], refs[-1]
-    rows, cells = out_ref.shape
-    for h, sums in enumerate(arrived_sums(received, cells)):
+    for h in range(cells // LO):
         a, b, c = (2 * h * rows + i * rows for i in range(3))
-        out_ref[:, h * LO : (h + 1) * LO] = (acc_ref[a:b] + acc_ref[b:c]) + sums
-
-
-def arrive_kernel(merged_ref, *refs):
-    received, out_ref = refs[:-1], refs[-1]
-    for h, sums in enumerate(arrived_sums(received, out_ref.shape[1])):
-        here = slice(h * LO, (h + 1) * LO)
-        out_ref[:, here] = merged_ref[:, here] + sums
+        out_ref[:, h * LO : (h + 1) * LO] = (acc_ref[a:b] + acc_ref[b:c]) + (sums[a:b] + sums[b:c])
 
 
 def rotated(value, axis, steps):
@@ -204,7 +189,7 @@
     count = lax.axis_size("lev")
     paired = lax.axis_size("panel") % 2 == 0
     points = blocks * slots
-    early = 1
+    early = 2
     shape = jax.ShapeDtypeStruct
     parts = [rotated(weights, "lev", s) for s in range(1, count)]
     inputs = (
@@ -267,26 +252,14 @@
         compiler_params=PARAMS,
         name="local",
     )(u, dep, full, keep, acc)
-    result = shape((rows, cells), F32)
-    merged = pl.pallas_call(
-        merge_kernel,
-        out_shape=result,
-        in_specs=[VMEM] * blocks,
-        out_specs=VMEM,
-        cost_estimate=pl.CostEstimate(
-            flops=4 * rows * cells * points, bytes_accessed=8 * rows * cells, transcendentals=0
-        ),
-        compiler_params=PARAMS,
-        name="merge",
-    )(acc, *received[:-1])
     out = pl.pallas_call(
         arrive_kernel,
-        out_shape=result,
-        in_specs=[VMEM] * 2,
+        out_shape=shape((rows, cells), F32),
+        in_specs=[VMEM] * (1 + blocks),
         out_specs=VMEM,
         compiler_params=PARAMS,
         name="arrive",
-    )(merged, received[-1])
+    )(acc, *received)
     return out.reshape(fields, levels, cells)
 
 

time: 11.5 us -> 11.6 us (level)
  the two profiles are of different devices: /device:TPU:0 before, /device:TPU:1 now
where the time goes in v9:
time: 11.6 us; the launch traced here: 11.4 us
  Pallas kernels  5.58 us (48%)
  starting transfers between devices  5.43 us (47%)
  waiting for transfers between devices  0.36 us (3%)
    ppermute x3, starting transfers between devices, rotated(): lax.ppermute(value, axis, [(i, (i + steps) % count) for i in range(count)])  4.11 us
    pallas_call x1, Pallas kernels, body(): pl.pallas_call(lambda *refs: local_kernel(early, count, *refs), out_shape...  2.24 us
    pallas_call x1, Pallas kernels, body(): pl.pallas_call(lambda *refs: prepare_kernel(levels, early, *refs), out_sh...  2.03 us
    ppermute x2, starting transfers between devices, racetrack(): return lax.ppermute(value, ('panel', 'tile'), route)  1.31 us
    pallas_call x1, Pallas kernels, body(): pl.pallas_call(arrive_kernel, out_shape=shape((rows, cells), F32), in_spe...  1.14 us
    ppermute x3, waiting for transfers between devices, rotated(): lax.ppermute(value, axis, [(i, (i + steps) % count) for i in range(count)])  0.36 us
  transfers between devices with their start and end apart: 5, of which 1 were waited for; matrix products, arithmetic and copies ran while one was open for 0% of the time, Pallas kernels for 37%

profile of v9, /device:TPU:1, one launch (start us, length us, event | category | flops | bytes accessed | tf_op | source)
XLA Modules:
  0.0 11.4 jit_solution(8765287389122557278)
XLA Ops:
  0.0 2.0 %collective-permute-start = (f32[4,1024]{1,0:T(4,128)}, f32[4,1024]{1,0:T(4,128)S(1)}, u32[]{:S(2)}, u32[]{:S(2)}) collective-permute-start(f32[4,1024]{1,0:T(4,128)} %refs_1_.1), channel_id=1, source_target_pairs={{0,1},{1,0},{2,3},{3,2},{4,5},{5,4},{6,7},{7,6},{8,9},{9,8},{10,11... | collective-permute-start | bytes 49160 | tf_op jit(solution)/shard_map/ppermute | solution.py:170
  2.0 2.0 %prepare.1 = (f32[40,2048]{1,0:T(8,128)S(1)}, f32[4,1024]{1,0:T(4,128)S(1)}, s32[4,2048]{1,0:T(4,128)S(1)}, f32[4,2048]{1,0:T(4,128)S(1)}, f32[48,512]{1,0:T(8,1...) custom-call(f32[40,2048]{1,0:T(8,128)} %bitcast.4, ...), custom_call_target="tpu_custom_call" | custom-call | flops 167772160 | bytes 655360 | tf_op jit(solution)/shard_map/prepare/pallas_call | solution.py:200
  4.1 0.0 collective-permute-done.refs_5_
  4.1 0.2 %send.1 = (f32[48,128]{1,0:T(8,128)S(1)}, f32[48,128]{1,0:T(8,128)S(1)}, f32[48,128]{1,0:T(8,128)S(1)}, f32[48,128]{1,0:T(8,128)S(1)}, f32[4,2048]{1,0:T(4,128)S(1)}) custom-call(f32[48,512]{1,0:T(8,128)S(1)} %get-tuple-element.21.refs_0_, s32[4,128]{1,0:T(4,128)S(1)} %get-tuple-element.22.refs_1_, s32[4,128]{1,0:T(4,128)S(1)} %get-tuple-element.23.refs_2_, ...), custom_call_target="tpu_custom_call" | custom-call | tf_op jit(solution)/shard_map/send/pallas_call | solution.py:226
  4.3 1.3 %collective-permute-start.1 = (f32[48,128]{1,0:T(8,128)S(1)}, f32[48,128]{1,0:T(8,128)S(1)}, u32[]{:S(2)}, u32[]{:S(2)}) collective-permute-start(f32[48,128]{1,0:T(8,128)S(1)} %get-tuple-element.29), channel_id=1, source_target_pairs={{0,8},{2,0},{4,2},{6,4},{8,10},{10,12},{12,14},{14,6},{16,24},{18,... | collective-permute-start | bytes 73736 | tf_op jit(solution)/shard_map/ppermute | solution.py:181
  5.6 1.3 %collective-permute-start.2 = (f32[48,128]{1,0:T(8,128)S(1)}, f32[48,128]{1,0:T(8,128)S(1)}, u32[]{:S(2)}, u32[]{:S(2)}) collective-permute-start(f32[48,128]{1,0:T(8,128)S(1)} %get-tuple-element.30), channel_id=1, source_target_pairs={{0,8},{8,16},{16,24},{24,0},{1,9},{9,17},{17,25},{25,1},{2,10},{10... | collective-permute-start | bytes 73736 | tf_op jit(solution)/shard_map/ppermute | solution.py:170
  6.8 0.0 collective-permute-start.3
  6.8 0.8 %collective-permute-start.4 = (f32[48,128]{1,0:T(8,128)S(1)}, f32[48,128]{1,0:T(8,128)S(1)}, u32[]{:S(2)}, u32[]{:S(2)}) collective-permute-start(f32[48,128]{1,0:T(8,128)S(1)} %get-tuple-element.32), channel_id=1, source_target_pairs={{0,24},{8,0},{16,8},{24,16},{1,25},{9,1},{17,9},{25,17},{2,26},{10... | collective-permute-start | bytes 73736 | tf_op jit(solution)/shard_map/ppermute | solution.py:170
  7.7 2.2 %local.1.acc_ref = f32[640,256]{1,0:T(8,128)S(1)} custom-call(f32[40,2048]{1,0:T(8,128)S(1)} %get-tuple-element.19.refs_0_, s32[4,2048]{1,0:T(4,128)S(1)} %get-tuple-element.20.refs_1_, f32[4,2048]{1,0:T(4,128)S(1)} %get-tuple-element.26.refs_2_, f32[4,2048]{1,0:T(4,128)S(1)} %get-tuple-element.27.refs_3_, f32[640,256]{1,0:T(8,128)S(1)} %get-tuple-element.28.refs_4_), custom_call_target="tpu_custom_call" | custom-call | flops 2684354560 | bytes 655360 | tf_op jit(solution)/shard_map/local/pallas_call | solution.py:244
  9.9 0.0 collective-permute-done.1.refs_0_
  9.9 0.0 collective-permute-done.2.refs_1_
  9.9 0.0 collective-permute-done.3.refs_2_
  9.9 0.4 %collective-permute-done.4.refs_3_ = f32[48,128]{1,0:T(8,128)S(1)} collective-permute-done((f32[48,128]{1,0:T(8,128)S(1)}, f32[48,128]{1,0:T(8,128)S(1)}, u32[]{:S(2)}, u32[]{:S(2)}) %collective-permute-start.4) | collective-permute-done | bytes 24608 | tf_op jit(solution)/shard_map/ppermute | solution.py:170
  10.3 1.1 %arrive.1 = f32[40,2048]{1,0:T(8,128)} custom-call(f32[640,256]{1,0:T(8,128)S(1)} %local.1.acc_ref, f32[48,128]{1,0:T(8,128)S(1)} %collective-permute-done.1.refs_0_, f32[48,128]{1,0:T(8,128)S(1)} %collective-permute-done.2.refs_1_, f32[48,128]{1,0:T(8,128)S(1)} %collective-permute-done.3.refs_2_, f32[48,128]{1,0:T(8,128)S(1)} %collective-permute-done.4.refs_3_), custom_call_target="tpu_custom_call" | custom-call | tf_op jit(solution)/shard_map/arrive/pallas_call | solution.py:255
Async XLA Ops:
  0.0 4.1 %collective-permute-start = (f32[4,1024]{1,0:T(4,128)}, f32[4,1024]{1,0:T(4,128)S(1)}, u32[]{:S(2)}, u32[]{:S(2)}) collective-permute-start(f32[4,1024]{1,0:T(4,128)} %refs_1_.1), channel_id=1, source_target_pairs={{0,1},{1,0},{2,3},{3,2},{4,5},{5,4},{6,7},{7,6},{8,9},{9,8},{10,11... | collective-permute-start | bytes 49160 | tf_op jit(solution)/shard_map/ppermute | solution.py:170
  4.3 5.7 %collective-permute-start.1 = (f32[48,128]{1,0:T(8,128)S(1)}, f32[48,128]{1,0:T(8,128)S(1)}, u32[]{:S(2)}, u32[]{:S(2)}) collective-permute-start(f32[48,128]{1,0:T(8,128)S(1)} %get-tuple-element.29), channel_id=1, source_target_pairs={{0,8},{2,0},{4,2},{6,4},{8,10},{10,12},{12,14},{14,6},{16,24},{18,... | collective-permute-start | bytes 73736 | tf_op jit(solution)/shard_map/ppermute | solution.py:181
  5.6 4.4 %collective-permute-start.2 = (f32[48,128]{1,0:T(8,128)S(1)}, f32[48,128]{1,0:T(8,128)S(1)}, u32[]{:S(2)}, u32[]{:S(2)}) collective-permute-start(f32[48,128]{1,0:T(8,128)S(1)} %get-tuple-element.30), channel_id=1, source_target_pairs={{0,8},{8,16},{16,24},{24,0},{1,9},{9,17},{17,25},{25,1},{2,10},{10... | collective-permute-start | bytes 73736 | tf_op jit(solution)/shard_map/ppermute | solution.py:170
  6.8 3.1 %collective-permute-start.3 = (f32[48,128]{1,0:T(8,128)S(1)}, f32[48,128]{1,0:T(8,128)S(1)}, u32[]{:S(2)}, u32[]{:S(2)}) collective-permute-start(f32[48,128]{1,0:T(8,128)S(1)} %get-tuple-element.31), channel_id=1, source_target_pairs={{0,2},{2,4},{4,6},{6,14},{8,0},{10,8},{12,10},{14,12},{16,18},{18,... | collective-permute-start | bytes 73736 | tf_op jit(solution)/shard_map/ppermute | solution.py:181
  6.8 3.5 %collective-permute-start.4 = (f32[48,128]{1,0:T(8,128)S(1)}, f32[48,128]{1,0:T(8,128)S(1)}, u32[]{:S(2)}, u32[]{:S(2)}) collective-permute-start(f32[48,128]{1,0:T(8,128)S(1)} %get-tuple-element.32), channel_id=1, source_target_pairs={{0,24},{8,0},{16,8},{24,16},{1,25},{9,1},{17,9},{25,17},{2,26},{10... | collective-permute-start | bytes 73736 | tf_op jit(solution)/shard_map/ppermute | solution.py:170

commit v10 on v8

--- a/solution.py
+++ b/solution.py
@@ -271,22 +271,22 @@
     merged = pl.pallas_call(
         merge_kernel,
         out_shape=result,
-        in_specs=[VMEM] * blocks,
+        in_specs=[VMEM] * (blocks - 1),
         out_specs=VMEM,
         cost_estimate=pl.CostEstimate(
             flops=4 * rows * cells * points, bytes_accessed=8 * rows * cells, transcendentals=0
         ),
         compiler_params=PARAMS,
         name="merge",
-    )(acc, *received[:-1])
+    )(acc, *received[:-2])
     out = pl.pallas_call(
         arrive_kernel,
         out_shape=result,
-        in_specs=[VMEM] * 2,
+        in_specs=[VMEM] * 3,
         out_specs=VMEM,
         compiler_params=PARAMS,
         name="arrive",
-    )(merged, received[-1])
+    )(merged, *received[-2:])
     return out.reshape(fields, levels, cells)
 
 

time: 11.5 us -> 11.5 us (level)
  no operation moved by 1% of the time
where the time goes in v10:
time: 11.5 us; the launch traced here: 11.3 us
  Pallas kernels  5.76 us (50%)
  starting transfers between devices  5.25 us (46%)
  waiting for transfers between devices  0.23 us (2%)
    ppermute x3, starting transfers between devices, rotated(): lax.ppermute(value, axis, [(i, (i + steps) % count) for i in range(count)])  3.65 us
    pallas_call x1, Pallas kernels, body(): pl.pallas_call(lambda *refs: local_kernel(early, count, *refs), out_shape...  2.58 us
    pallas_call x1, Pallas kernels, body(): pl.pallas_call(lambda *refs: prepare_kernel(levels, early, *refs), out_sh...  1.7 us
    ppermute x2, starting transfers between devices, racetrack(): return lax.ppermute(value, ('panel', 'tile'), route)  1.6 us
    pallas_call x1, Pallas kernels, body(): pl.pallas_call(arrive_kernel, out_shape=result, in_specs=[VMEM] * 3, out_...  1.02 us
    pallas_call x1, Pallas kernels, body(): pl.pallas_call(merge_kernel, out_shape=result, in_specs=[VMEM] * (blocks...  0.3 us
  transfers between devices with their start and end apart: 5, of which 1 were waited for; matrix products, arithmetic and copies ran while one was open for 0% of the time, Pallas kernels for 41%

profile of v10, /device:TPU:0, one launch (start us, length us, event | category | flops | bytes accessed | tf_op | source)
XLA Modules:
  0.0 11.3 jit_solution(14982766733894457645)
XLA Ops:
  0.0 3.0 %collective-permute-start = (f32[4,1024]{1,0:T(4,128)}, f32[4,1024]{1,0:T(4,128)S(1)}, u32[]{:S(2)}, u32[]{:S(2)}) collective-permute-start(f32[4,1024]{1,0:T(4,128)} %refs_1_.1), channel_id=1, source_target_pairs={{0,1},{1,0},{2,3},{3,2},{4,5},{5,4},{6,7},{7,6},{8,9},{9,8},{10,11... | collective-permute-start | bytes 49160 | tf_op jit(solution)/shard_map/ppermute | solution.py:185
  3.0 1.7 %prepare.1 = (f32[40,2048]{1,0:T(8,128)S(1)}, f32[4,1024]{1,0:T(4,128)S(1)}, s32[4,2048]{1,0:T(4,128)S(1)}, f32[4,2048]{1,0:T(4,128)S(1)}, f32[48,512]{1,0:T(8,1...) custom-call(f32[40,2048]{1,0:T(8,128)} %bitcast.4, ...), custom_call_target="tpu_custom_call" | custom-call | flops 167772160 | bytes 655360 | tf_op jit(solution)/shard_map/prepare/pallas_call | solution.py:215
  4.7 0.2 %collective-permute-done.refs_5_ = f32[4,1024]{1,0:T(4,128)S(1)} collective-permute-done((f32[4,1024]{1,0:T(4,128)}, f32[4,1024]{1,0:T(4,128)S(1)}, u32[]{:S(2)}, u32[]{:S(2)}) %collective-permute-start) | collective-permute-done | bytes 16416 | tf_op jit(solution)/shard_map/ppermute | solution.py:185
  4.9 0.2 %send.1 = (f32[48,128]{1,0:T(8,128)S(1)}, f32[48,128]{1,0:T(8,128)S(1)}, f32[48,128]{1,0:T(8,128)S(1)}, f32[48,128]{1,0:T(8,128)S(1)}, f32[4,2048]{1,0:T(4,128)S(1)}) custom-call(f32[48,512]{1,0:T(8,128)S(1)} %get-tuple-element.21.refs_0_, s32[4,128]{1,0:T(4,128)S(1)} %get-tuple-element.22.refs_1_, s32[4,128]{1,0:T(4,128)S(1)} %get-tuple-element.23.refs_2_, ...), custom_call_target="tpu_custom_call" | custom-call | tf_op jit(solution)/shard_map/send/pallas_call | solution.py:241
  5.1 0.0 collective-permute-start.1
  5.1 0.6 %collective-permute-start.2 = (f32[48,128]{1,0:T(8,128)S(1)}, f32[48,128]{1,0:T(8,128)S(1)}, u32[]{:S(2)}, u32[]{:S(2)}) collective-permute-start(f32[48,128]{1,0:T(8,128)S(1)} %get-tuple-element.30), channel_id=1, source_target_pairs={{0,8},{8,16},{16,24},{24,0},{1,9},{9,17},{17,25},{25,1},{2,10},{10... | collective-permute-start | bytes 73736 | tf_op jit(solution)/shard_map/ppermute | solution.py:185
  5.7 1.6 %collective-permute-start.3 = (f32[48,128]{1,0:T(8,128)S(1)}, f32[48,128]{1,0:T(8,128)S(1)}, u32[]{:S(2)}, u32[]{:S(2)}) collective-permute-start(f32[48,128]{1,0:T(8,128)S(1)} %get-tuple-element.31), channel_id=1, source_target_pairs={{0,2},{2,4},{4,6},{6,14},{8,0},{10,8},{12,10},{14,12},{16,18},{18,... | collective-permute-start | bytes 73736 | tf_op jit(solution)/shard_map/ppermute | solution.py:196
  7.3 0.1 collective-permute-start.4
  7.4 2.6 %local.1.acc_ref = f32[640,256]{1,0:T(8,128)S(1)} custom-call(f32[40,2048]{1,0:T(8,128)S(1)} %get-tuple-element.19.refs_0_, s32[4,2048]{1,0:T(4,128)S(1)} %get-tuple-element.20.refs_1_, f32[4,2048]{1,0:T(4,128)S(1)} %get-tuple-element.26.refs_2_, f32[4,2048]{1,0:T(4,128)S(1)} %get-tuple-element.27.refs_3_, f32[640,256]{1,0:T(8,128)S(1)} %get-tuple-element.28.refs_4_), custom_call_target="tpu_custom_call" | custom-call | flops 2684354560 | bytes 655360 | tf_op jit(solution)/shard_map/local/pallas_call | solution.py:259
  9.9 0.0 collective-permute-done.1.refs_0_
  10.0 0.0 collective-permute-done.2.refs_1_
  10.0 0.3 %merge.1.merged_ref = f32[40,2048]{1,0:T(8,128)S(1)} custom-call(f32[640,256]{1,0:T(8,128)S(1)} %local.1.acc_ref, f32[48,128]{1,0:T(8,128)S(1)} %collective-permute-done.1.refs_0_, f32[48,128]{1,0:T(8,128)S(1)} %collective-permute-done.2.refs_1_), custom_call_target="tpu_custom_call" | custom-call | flops 167772160 | bytes 655360 | tf_op jit(solution)/shard_map/merge/pallas_call | solution.py:271
  10.3 0.0 collective-permute-done.3.refs_0_
  10.3 0.0 collective-permute-done.4.refs_1_
  10.3 1.0 %arrive.1 = f32[40,2048]{1,0:T(8,128)} custom-call(f32[40,2048]{1,0:T(8,128)S(1)} %merge.1.merged_ref, f32[48,128]{1,0:T(8,128)S(1)} %collective-permute-done.3.refs_0_, f32[48,128]{1,0:T(8,128)S(1)} %collective-permute-done.4.refs_1_), custom_call_target="tpu_custom_call" | custom-call | tf_op jit(solution)/shard_map/arrive/pallas_call | solution.py:282
Async XLA Ops:
  0.0 4.9 %collective-permute-start = (f32[4,1024]{1,0:T(4,128)}, f32[4,1024]{1,0:T(4,128)S(1)}, u32[]{:S(2)}, u32[]{:S(2)}) collective-permute-start(f32[4,1024]{1,0:T(4,128)} %refs_1_.1), channel_id=1, source_target_pairs={{0,1},{1,0},{2,3},{3,2},{4,5},{5,4},{6,7},{7,6},{8,9},{9,8},{10,11... | collective-permute-start | bytes 49160 | tf_op jit(solution)/shard_map/ppermute | solution.py:185
  5.1 4.9 %collective-permute-start.1 = (f32[48,128]{1,0:T(8,128)S(1)}, f32[48,128]{1,0:T(8,128)S(1)}, u32[]{:S(2)}, u32[]{:S(2)}) collective-permute-start(f32[48,128]{1,0:T(8,128)S(1)} %get-tuple-element.29), channel_id=1, source_target_pairs={{0,8},{2,0},{4,2},{6,4},{8,10},{10,12},{12,14},{14,6},{16,24},{18,... | collective-permute-start | bytes 73736 | tf_op jit(solution)/shard_map/ppermute | solution.py:196
  5.1 4.9 %collective-permute-start.2 = (f32[48,128]{1,0:T(8,128)S(1)}, f32[48,128]{1,0:T(8,128)S(1)}, u32[]{:S(2)}, u32[]{:S(2)}) collective-permute-start(f32[48,128]{1,0:T(8,128)S(1)} %get-tuple-element.30), channel_id=1, source_target_pairs={{0,8},{8,16},{16,24},{24,0},{1,9},{9,17},{17,25},{25,1},{2,10},{10... | collective-permute-start | bytes 73736 | tf_op jit(solution)/shard_map/ppermute | solution.py:185
  5.7 4.6 %collective-permute-start.3 = (f32[48,128]{1,0:T(8,128)S(1)}, f32[48,128]{1,0:T(8,128)S(1)}, u32[]{:S(2)}, u32[]{:S(2)}) collective-permute-start(f32[48,128]{1,0:T(8,128)S(1)} %get-tuple-element.31), channel_id=1, source_target_pairs={{0,2},{2,4},{4,6},{6,14},{8,0},{10,8},{12,10},{14,12},{16,18},{18,... | collective-permute-start | bytes 73736 | tf_op jit(solution)/shard_map/ppermute | solution.py:196
  7.3 3.0 %collective-permute-start.4 = (f32[48,128]{1,0:T(8,128)S(1)}, f32[48,128]{1,0:T(8,128)S(1)}, u32[]{:S(2)}, u32[]{:S(2)}) collective-permute-start(f32[48,128]{1,0:T(8,128)S(1)} %get-tuple-element.32), channel_id=1, source_target_pairs={{0,24},{8,0},{16,8},{24,16},{1,25},{9,1},{17,9},{25,17},{2,26},{10... | collective-permute-start | bytes 73736 | tf_op jit(solution)/shard_map/ppermute | solution.py:185
